TPU v7x, 32 devices: a whole 2x2x4 slice. The times are simulated.
32 devices in a mesh: tm: 8 (over y, x, core), space: 4 (over z).
Axes of the slice: x: 2, y: 2, z: 4, core: 2. Of those that a mesh axis runs over, the one named last changes fastest.
Arguments:
- c_state: float32 [8, 3, 2, 512, 1024], P('tm', None, None, 'space'), may hold values from -4 to 4
- init: float32 [3, 2, 512, 1024], P(None, None, 'space'), may hold values from -4 to 4
Outputs:
- new_c: float32 [8, 3, 2, 512, 1024], P('tm', None, None, 'space')
- residual: float32 [8, 3, 2, 512, 1024], P('tm', None, None, 'space')
All inputs are finite; a program needn't handle non-finite values.
Results may differ from a plain program's by a relative error of at most 0.00019.
Values sent between devices are 32-bit elements; how exact they have to be, the bound alone decides.
A program may use at most 128 MiB of HBM per device.

v0:
```python
import math

import jax
import jax.numpy as jnp
from jax import lax
from jax.sharding import PartitionSpec as P

CF = 2


CORIOLIS = 1.0
HYPERDIFFUSION = 0.25
COURANT = 0.4
PRECISE = lax.Precision.HIGHEST


def passed_along(value, axis, steps):
    count = lax.axis_size(axis)
    initial, last = (max(0, -steps), min(count, count - steps))
    return lax.ppermute(value, axis, [(source, source + steps) for source in range(initial, last)])


def entering(value, axis, join, neutral):
    count, mine = (lax.axis_size(axis), lax.axis_index(axis))
    pieces = jax.tree.map(lambda part: lax.all_gather(part, axis), value)
    running = jax.tree.map(
        lambda part, zero: jnp.full_like(part, 0) + jnp.asarray(zero, part.dtype), value, neutral
    )

    def step(position, running):
        longer = join(running, jax.tree.map(lambda part: part[position], pieces))
        return jax.tree.map(lambda new, old: jnp.where(position < mine, new, old), longer, running)

    return lax.fori_loop(0, count - 1, step, running)


def times_imag(values):
    return jnp.stack([-values[..., 1, :, :], values[..., 0, :, :]], axis=-3)


def divide_imag(values):
    return jnp.stack([values[..., 1, :, :], -values[..., 0, :, :]], axis=-3)


def operator_m(x_wind, y_wind, tilted, wave_x, wave_y):
    return (
        CORIOLIS * y_wind - wave_x * tilted,
        -CORIOLIS * x_wind - wave_y * tilted,
        wave_x * x_wind + wave_y * y_wind,
    )


def prop_factors(steps, wave_x, wave_y, grid_size):
    time_step = COURANT / grid_size
    squared = wave_x * wave_x + wave_y * wave_y
    frequency = jnp.sqrt(CORIOLIS * CORIOLIS + squared)
    ratio = squared / (0.25 * grid_size * grid_size)
    log_damp = -HYPERDIFFUSION * (ratio * ratio) * (ratio * ratio)
    phase_angle = frequency * (steps * time_step)
    first_coef = jnp.sin(phase_angle) / frequency
    second_coef = (1.0 - jnp.cos(phase_angle)) / (frequency * frequency)
    damping = jnp.exp(steps * log_damp)
    return (first_coef, second_coef, damping)


def apply_factors(state, factors, wave_x, wave_y):
    first_coef, second_coef, damping = factors
    base = (state[..., 0, :, :, :], state[..., 1, :, :, :], times_imag(state[..., 2, :, :, :]))
    applied = operator_m(base[0], base[1], base[2], wave_x, wave_y)
    applied_twice = operator_m(applied[0], applied[1], applied[2], wave_x, wave_y)
    results = [
        (base[field_id] + first_coef * applied[field_id] + second_coef * applied_twice[field_id])
        * damping
        for field_id in range(3)
    ]
    return jnp.stack([results[0], results[1], divide_imag(results[2])], axis=-4)


def propagate(state, steps, wave_x, wave_y, grid_size):
    return apply_factors(state, prop_factors(steps, wave_x, wave_y, grid_size), wave_x, wave_y)


def dft_block(length, direction):
    counter = jnp.arange(length, dtype=jnp.int32)
    phase_turns = counter[:, None] * counter[None, :] % length
    phase_angle = 2.0 * math.pi / length * phase_turns.astype(jnp.float32)
    cosine = jnp.cos(phase_angle)
    sine_part = direction * jnp.sin(phase_angle)
    top_rows = jnp.stack([cosine, -sine_part], axis=1)
    bottom_rows = jnp.stack([sine_part, cosine], axis=1)
    return jnp.stack([top_rows, bottom_rows], axis=0)


def twiddle_pair(row_len, col_len, grid_size, direction):
    phase_turns = (
        jnp.arange(row_len, dtype=jnp.int32)[:, None]
        * jnp.arange(col_len, dtype=jnp.int32)[None, :]
        % grid_size
    )
    phase_angle = 2.0 * math.pi / grid_size * phase_turns.astype(jnp.float32)
    return (jnp.cos(phase_angle), direction * jnp.sin(phase_angle))


def rotate_values(values, cosine, sine_part):
    real_part = values[:, 0]
    imag_part = values[:, 1]
    return jnp.stack(
        [real_part * cosine - imag_part * sine_part, real_part * sine_part + imag_part * cosine],
        axis=1,
    )


def make_tables(grid_size, ky_local, ky_start):
    first_len = 1 << (grid_size.bit_length() - 1) // 2
    second_len = grid_size // first_len
    counter = jnp.arange(grid_size, dtype=jnp.int32)
    wave_x = jnp.where(counter < grid_size // 2, counter, counter - grid_size).astype(jnp.float32)
    wave_y = (ky_start + jnp.arange(ky_local, dtype=jnp.int32)).astype(jnp.float32)[:, None]
    keep_mask = ((jnp.abs(wave_x) <= grid_size // 3)[None, :] & (wave_y <= grid_size // 3)).astype(
        jnp.float32
    )
    half_len = grid_size // 2
    row_index = jnp.arange(half_len, dtype=jnp.int32)
    phase_turns = row_index[:, None] * counter[None, :] % grid_size
    phase_angle = 2.0 * math.pi / grid_size * phase_turns.astype(jnp.float32)
    weight = jnp.where(row_index == 0, 1.0, 2.0).astype(jnp.float32)[:, None] / grid_size
    inverse_y = jnp.stack([weight * jnp.cos(phase_angle), -weight * jnp.sin(phase_angle)])
    forward_y = jnp.stack([jnp.cos(phase_angle), -jnp.sin(phase_angle)]) / grid_size
    inv_cos, inv_sin = twiddle_pair(first_len, second_len, grid_size, 1.0)
    fwd_cos, fwd_sin = twiddle_pair(first_len, second_len, grid_size, -1.0)
    return {
        "wave_x": wave_x,
        "wave_y": wave_y,
        "keep_mask": keep_mask,
        "inverse_y": inverse_y,
        "forward_y": forward_y,
        "inv_first": dft_block(first_len, 1.0),
        "inv_second": dft_block(second_len, 1.0),
        "fwd_first": dft_block(first_len, -1.0),
        "fwd_second": dft_block(second_len, -1.0),
        "inv_cos": inv_cos,
        "inv_sin": inv_sin,
        "fwd_cos": fwd_cos,
        "fwd_sin": fwd_sin,
        "first_len": first_len,
        "second_len": second_len,
        "grid_size": grid_size,
        "ky_local": ky_local,
        "ky_start": ky_start,
        "one_step": prop_factors(1.0, wave_x, wave_y, grid_size),
    }


def inverse_columns(fields, tables):
    count_fields = fields.shape[0]
    ky_local = fields.shape[2]
    blocks = fields.reshape(count_fields, 2, ky_local, tables["first_len"], tables["second_len"])
    section_one = jnp.einsum("dkcn,fcjnb->fdjkb", tables["inv_first"], blocks, precision=PRECISE)
    section_one = rotate_values(section_one, tables["inv_cos"], tables["inv_sin"])
    section_two = jnp.einsum(
        "emdb,fdjkb->fejkm", tables["inv_second"], section_one, precision=PRECISE
    )
    return section_two.reshape(count_fields, 2, ky_local, tables["grid_size"])


def forward_columns(fields, tables):
    count_fields = fields.shape[0]
    ky_local = fields.shape[2]
    blocks = fields.reshape(count_fields, 2, ky_local, tables["first_len"], tables["second_len"])
    section_one = jnp.einsum("dmcb,fcjab->fdjam", tables["fwd_second"], blocks, precision=PRECISE)
    section_one = rotate_values(section_one, tables["fwd_cos"], tables["fwd_sin"])
    section_two = jnp.einsum(
        "ekda,fdjam->fejkm", tables["fwd_first"], section_one, precision=PRECISE
    )
    return section_two.reshape(count_fields, 2, ky_local, tables["grid_size"])


def fine_step(state, tables):
    wave_x = tables["wave_x"]
    wave_y = tables["wave_y"]
    grid_size = tables["grid_size"]
    time_step = COURANT / grid_size
    x_wind, y_wind, height = (state[0], state[1], state[2])
    vortex = times_imag(wave_x * y_wind - wave_y * x_wind)
    rotated = inverse_columns(jnp.stack([x_wind, y_wind, height, vortex]), tables)
    physical = jnp.einsum(
        "fclx,cly->fxy",
        lax.all_to_all(rotated, "space", split_axis=3, concat_axis=2, tiled=True),
        tables["inverse_y"],
        precision=PRECISE,
    )
    east_flow, north_flow, depth_field, spin_field = (
        physical[0],
        physical[1],
        physical[2],
        physical[3],
    )
    products = jnp.stack(
        [
            spin_field * north_flow,
            spin_field * east_flow,
            0.5 * (east_flow * east_flow + north_flow * north_flow),
            depth_field * east_flow,
            depth_field * north_flow,
        ]
    )
    partial_y = jnp.einsum("fxy,cly->fclx", products, tables["forward_y"], precision=PRECISE)
    modes = forward_columns(
        lax.all_to_all(partial_y, "space", split_axis=2, concat_axis=3, tiled=True), tables
    )
    tend_x = modes[0] - times_imag(wave_x * modes[2])
    tend_y = -modes[1] - times_imag(wave_y * modes[2])
    tend_h = -times_imag(wave_x * modes[3] + wave_y * modes[4])
    tendency = jnp.stack([tend_x, tend_y, tend_h]) * tables["keep_mask"]
    return apply_factors(state + time_step * tendency, tables["one_step"], wave_x, wave_y)


def shards(c_state, init):
    ky_local = c_state.shape[3]
    grid_size = c_state.shape[4]
    tables = make_tables(grid_size, ky_local, lax.axis_index("space") * ky_local)
    wave_x = tables["wave_x"]
    wave_y = tables["wave_y"]
    coarse_steps = float(CF)
    coarse_factors = prop_factors(coarse_steps, wave_x, wave_y, grid_size)
    own_slab = lax.axis_index("tm")
    leading = own_slab == 0
    shifted = passed_along(c_state, "tm", 1)
    previous = jnp.where(leading, init[None], shifted)[0]
    current = previous
    for repeat in range(CF):
        current = fine_step(current, tables)
    residual = current - c_state[0]
    offset = current - apply_factors(previous, coarse_factors, wave_x, wave_y)

    def compose(earlier, latter):
        return (
            propagate(earlier[0], latter[1] * coarse_steps, wave_x, wave_y, grid_size) + latter[0],
            earlier[1] + latter[1],
        )

    identity = (jnp.zeros_like(offset), jnp.zeros((), jnp.float32))
    summed, covered = entering((offset, jnp.ones((), jnp.float32)), "tm", compose, identity)
    before = propagate(init, covered * coarse_steps, wave_x, wave_y, grid_size) + summed
    corrected = apply_factors(before, coarse_factors, wave_x, wave_y) + offset
    return (corrected[None], residual[None])


def solution(mesh):
    placed = (P("tm", None, None, "space", None), P(None, None, "space", None))
    return jax.shard_map(
        shards,
        mesh=mesh,
        in_specs=placed,
        out_specs=(P("tm", None, None, "space", None), P("tm", None, None, "space", None)),
        check_vma=False,
    )
```

profile of v0, /device:TPU:0, one launch (start us, length us, event | category | flops | bytes accessed | tf_op | source)
XLA Modules:
  0.0 958.8 jit_solution(17517809294650942514)
XLA Ops:
  9.6 4.0 collective-permute-start
  13.6 3.5 copy.151
  17.6 5.6 fusion.184
  30.4 3.9 fusion.106
  35.8 6.6 fusion.99
  42.9 5.3 copy.160
  48.2 5.7 all-to-all-start
  53.9 9.2 fusion.176
  63.1 10.0 %broadcast_multiply_fusion = (f32[1,512,1024]{2,1,0:T(8,128)}, f32[1,512,1024]{2,1,0:T(8,128)}) fusion(f32[512]{0:T(512)S(1)} %fusion.234, f32[512]{0:T(512)S(1)} %select_multiply_fusion), kind=kLoop, calls=%fused_computation.282 | loop fusion | flops 8388608 | bytes 4198400 | tf_op jit(solution)/shard_map/mul | solution.py:127
  73.1 63.2 %all-to-all-done = f32[4,2,128,1024]{2,1,0,3:T(2,128)} async-done(((f32[4,2,128,1024]{2,1,0,3:T(2,128)}), f32[4,2,128,1024]{2,1,0,3:T(2,128)}, u32[]{:S(2)}, u32[]{:S(2)}) %all-to-all-start) | async-done | bytes 4194336 | tf_op jit(solution)/shard_map/all_to_all | solution.py:188
  139.8 13.4 %fusion.107 = f32[4,256,1024]{2,1,0:T(8,128)S(1)} fusion(f32[1,512,1024]{2,1,0:T(8,128)S(1)} %copy-done.29, f32[1,512,1024]{2,1,0:T(8,128)S(1)} %copy-done.31, f32[4,2,4,32,8,128]{5,4,3,2,1,0:T(8,128)S(1)} %bitcast.508), kind=kOutput, calls=%fused_computation.128 | convolution fusion | flops 12885950464 | bytes 12582912 | tf_op jit(solution)/shard_map/fclx,cly->fxy/dot_general | solution.py:186
  156.3 17.1 %fusion.76 = f32[5,2,512,256]{3,2,0,1:T(8,128)S(1)} fusion(f32[5,256,1024]{2,1,0:T(8,128)S(1)} %multiply_dynamic-update-slice_fusion.5, f32[1,512,1024]{2,1,0:T(8,128)S(1)} %copy-done.35, f32[1,512,1024]{2,1,0:T(8,128)S(1)} %copy-done.33), kind=kOutput, calls=%fused_computation.117 | convolution fusion | flops 16108224512 | bytes 14680064 | tf_op jit(solution)/shard_map/fxy,cly->fclx/dot_general | solution.py:207
  173.4 6.4 copy.163
  179.8 5.0 all-to-all-start.1
  186.2 114.8 %all-to-all-done.1 = f32[5,2,512,256]{3,1,0,2:T(2,128)} async-done(((f32[5,2,512,256]{3,1,0,2:T(2,128)}), f32[5,2,512,256]{3,1,0,2:T(2,128)}, u32[]{:S(2)}, u32[]{:S(2)}) %all-to-all-start.1) | async-done | bytes 5242912 | tf_op jit(solution)/shard_map/all_to_all | solution.py:209
  300.9 5.4 copy.164
  306.3 5.9 copy.165
  312.2 7.0 fusion.81
  321.0 8.3 fusion.84
  343.3 3.9 fusion.105
  349.1 6.4 fusion.102
  359.3 97.0 %all_to_all.66 = f32[4,2,128,1024]{2,1,0,3:T(2,128)S(1)} all-to-all(f32[4,2,128,1024]{2,1,0,3:T(2,128)S(1)} %copy.181), channel_id=1, replica_groups=mesh['tm'=8,'space'=4] {'space'}, dimensions={3} | all-to-all | bytes 8388608 | tf_op jit(solution)/shard_map/all_to_all | solution.py:188
  458.5 13.4 %fusion.110 = f32[4,256,1024]{2,1,0:T(8,128)S(1)} fusion(f32[1,512,1024]{2,1,0:T(8,128)S(1)} %copy-done.30, f32[1,512,1024]{2,1,0:T(8,128)S(1)} %copy-done.32, f32[4,2,4,32,8,128]{5,4,3,2,1,0:T(8,128)S(1)} %bitcast.507), kind=kOutput, calls=%fused_computation.129 | convolution fusion | flops 12885950464 | bytes 12582912 | tf_op jit(solution)/shard_map/fclx,cly->fxy/dot_general | solution.py:186
  475.2 16.9 %fusion.87 = f32[5,2,512,256]{3,2,0,1:T(8,128)S(1)} fusion(f32[5,256,1024]{2,1,0:T(8,128)S(1)} %multiply_dynamic-update-slice_fusion, f32[1,512,1024]{2,1,0:T(8,128)S(1)} %copy-done.36, f32[1,512,1024]{2,1,0:T(8,128)S(1)} %copy-done.34), kind=kOutput, calls=%fused_computation.120 | convolution fusion | flops 16108224512 | bytes 14680064 | tf_op jit(solution)/shard_map/fxy,cly->fclx/dot_general | solution.py:207
  492.1 6.4 copy.184
  498.5 5.2 all-to-all-start.3
  505.9 113.9 %all-to-all-done.3 = f32[5,2,512,256]{3,1,0,2:T(2,128)} async-done(((f32[5,2,512,256]{3,1,0,2:T(2,128)}), f32[5,2,512,256]{3,1,0,2:T(2,128)}, u32[]{:S(2)}, u32[]{:S(2)}) %all-to-all-start.3) | async-done | bytes 5242912 | tf_op jit(solution)/shard_map/all_to_all | solution.py:209
  619.8 5.4 copy.185
  625.1 5.9 copy.186
  631.0 7.2 fusion.92
  640.1 8.4 fusion.95
  666.1 44.0 %all-reduce = f32[8]{0:T(128)S(1)} all-reduce(f32[8]{0:T(128)S(1)} %dynamic-update-slice), channel_id=1, replica_groups=mesh['tm'=8,'space'=4] {'tm'}, use_global_device_ids=true, to_apply=%add | all-reduce | flops 8 | bytes 64
  712.6 3.5 copy.201
  716.1 105.1 %all-gather.2.cloned.1.call-done = f32[8,3,2,128,1024]{4,3,2,1,0:T(8,128)} async-done(((f32[1,3,2,128,1024]{4,3,2,1,0:T(8,128)}), f32[8,3,2,128,1024]{4,3,2,1,0:T(8,128)}) %all-gather.2.cloned.1.call-update) | async-done | bytes 25165840 | tf_op jit(solution)/shard_map/all_gather | solution.py:25
  821.3 111.1 %while.21 = (s32[]{:T(128)}, f32[3,2,128,1024]{3,2,1,0:T(8,128)S(1)}, f32[]{:T(128)}, s32[]{:T(128)}, f32[8]{0:T(128)S(1)}, /*index=5*/f32[8,3,2,128,1024]{4,3,2...) while((s32[]{:T(128)}, ...), condition=%wide.region_1.2_spmd.clone.clone.clone.clone, body=%wide.region_0.1_spmd.clone.clone.clone.clone.sunk | while | flops 17573508 | bytes 46684968 | solution.py:34
  823.3 3.4 fusion.271
  832.4 4.0 fusion.275
  839.2 3.4 fusion.271
  848.2 4.0 fusion.275
  855.1 3.4 fusion.271
  864.1 4.0 fusion.275
  871.0 3.4 fusion.271
  880.0 4.0 fusion.275
  886.8 3.4 fusion.271
  895.9 4.0 fusion.275
  902.7 3.4 fusion.271
  911.8 4.0 fusion.275
  927.6 4.0 fusion.275
  (324 shorter events, 136.6 us)
Async XLA Ops:
  9.6 7.6 copy-start.16
  9.6 13.6 %collective-permute-start = (f32[1,3,2,128,1024]{3,4,2,1,0:T(8,128)S(1)}, f32[1,3,2,128,1024]{3,4,2,1,0:T(8,128)}, u32[]{:S(2)}, u32[]{:S(2)}) collective-permute-start(f32[1,3,2,128,1024]{3,4,2,1,0:T(8,128)S(1)} %copy.153), channel_id=1, source_target_pairs={{0,4},{4,8},{8,12},{12,16},{16,20},{20,24},{24,28},{1,5},{5,9},{9,... | collective-permute-start | bytes 9437192 | tf_op jit(solution)/shard_map/ppermute | solution.py:20
  17.2 6.0 copy-start.3
  17.2 6.4 copy-start.42
  17.2 6.4 copy-start.40
  23.2 3.1 copy-start.6
  23.2 3.2 copy-start.8
  23.2 3.2 copy-start.10
  48.2 88.1 %all-to-all-start = ((f32[4,2,128,1024]{2,1,0,3:T(2,128)}), f32[4,2,128,1024]{2,1,0,3:T(2,128)}, u32[]{:S(2)}, u32[]{:S(2)}) async-start(f32[4,2,128,1024]{2,1,0,3:T(2,128)} %copy.160), calls=%async_computation | async-start | bytes 8388608 | tf_op jit(solution)/shard_map/all_to_all | solution.py:188
  136.3 3.2 copy-start.29
  136.3 3.5 copy-start.31
  154.1 1.6 copy-start.33
  154.1 2.2 copy-start.35
  179.8 121.1 %all-to-all-start.1 = ((f32[5,2,512,256]{3,1,0,2:T(2,128)}), f32[5,2,512,256]{3,1,0,2:T(2,128)}, u32[]{:S(2)}, u32[]{:S(2)}) async-start(f32[5,2,512,256]{3,1,0,2:T(2,128)} %copy.163), calls=%async_computation.1 | async-start | bytes 10485760 | tf_op jit(solution)/shard_map/all_to_all | solution.py:209
  336.1 1.3 copy-start.14
  340.3 1.3 copy-start.18
  456.3 1.6 copy-start.30
  456.3 2.2 copy-start.32
  473.0 1.6 copy-start.34
  473.0 2.2 copy-start.36
  498.5 5.2 copy-start.39
  498.5 121.3 %all-to-all-start.3 = ((f32[5,2,512,256]{3,1,0,2:T(2,128)}), f32[5,2,512,256]{3,1,0,2:T(2,128)}, u32[]{:S(2)}, u32[]{:S(2)}) async-start(f32[5,2,512,256]{3,1,0,2:T(2,128)} %copy.184), calls=%async_computation.3 | async-start | bytes 10485760 | tf_op jit(solution)/shard_map/all_to_all | solution.py:209
  503.7 317.6 %all-gather.2.cloned.1.call-start = ((), (), s32[]{:S(2)}) async-start(), calls=%async_computation.4 | async-start | bytes 28311552 | tf_op jit(solution)/shard_map/all_gather | solution.py:25
  653.5 1.2 copy-start.19
  653.5 1.3 copy-start.21
  653.5 1.7 copy-start.25
  656.5 1.9 copy-start.17
  656.5 2.2 copy-start.26
  656.5 2.5 copy-start.27
  656.5 2.8 copy-start.28
  661.5 2.6 copy-start.4
  821.2 111.2 %copy-start.41 = (f32[1024]{0:T(1024)S(1)}, f32[1024]{0:T(1024)}, u32[]{:S(2)}) copy-start(f32[1024]{0:T(1024)} %copy-done.40) | copy-start | bytes 12292
  821.2 111.2 %copy-start.43 = (f32[128]{0:T(128)S(1)}, f32[128]{0:T(128)}, u32[]{:S(2)}) copy-start(f32[128]{0:T(128)} %copy-done.42) | copy-start | bytes 1540
  827.0 1.3 copy-start.2
  842.9 1.3 copy-start.2
  858.8 1.3 copy-start.2
  874.7 1.3 copy-start.2
  890.5 1.3 copy-start.2
  906.4 1.3 copy-start.2
  922.3 1.3 copy-start.2
  934.7 4.1 copy-start.22
  934.7 4.1 copy-start.23
  934.7 4.1 copy-start.24
  941.2 3.3 copy-start.37
  941.2 3.3 copy-start.38
  941.2 3.6 copy-start.15
  945.1 1.3 copy-start.11
  947.2 1.9 copy-start.5
  (20 other events, 21.8 us)
Sparse Core Ops, SparseCore 0:
  664.2 156.9 all-gather.1
where the time goes:
time: 970 us; the launch traced here: 959 us
  waiting for transfers between devices  397 us (41%)
  other arithmetic  154 us (16%)
  blocking collectives  141 us (15%)
  matrix products  113 us (12%)
  local copies, waits for them, and re-layouts  104 us (11%)
  starting transfers between devices  20 us (2%)
  between operations  15.3 us (2%)
  loops' own time  15.2 us (2%)
    all_to_all x2, waiting for transfers between devices, fine_step(): lax.all_to_all(partial_y, 'space', split_axis=2, concat_axis=3, tiled=True)  229 us
    all_gather x1, waiting for transfers between devices, entering(): pieces = jax.tree.map(lambda part: lax.all_gather(part, axis), value)  105 us
    all_to_all x1, blocking collectives, fine_step(): lax.all_to_all(rotated, 'space', split_axis=3, concat_axis=2, tiled=True)  97 us
    all_to_all x1, waiting for transfers between devices, fine_step(): lax.all_to_all(rotated, 'space', split_axis=3, concat_axis=2, tiled=True)  63.2 us
    unnamed x1, blocking collectives  44 us
    dot_general x2, matrix products, fine_step(): jnp.einsum('fxy,cly->fclx', products, tables['forward_y'], precision=PREC...  34 us
    div x9, other arithmetic, prop_factors(): first_coef = jnp.sin(phase_angle) / frequency  31.5 us
    mul x20, other arithmetic, apply_factors(): (base[field_id] + first_coef * applied[field_id] + second_coef * applied_...  30.2 us
  transfers between devices with their start and end apart: 5, of which 4 were waited for; matrix products, arithmetic and copies ran while one was open for 4% of the time, Pallas kernels for 0%

commit v1 on v0

v1 whole, which is shorter than its diff:
```python
import math

import jax
import jax.numpy as jnp
import numpy as np
from jax import lax
from jax.experimental import pallas as pl
from jax.experimental.pallas import tpu as pltpu
from jax.sharding import Mesh, PartitionSpec as P

CF = 2
CORIOLIS = 1.0
HYPERDIFFUSION = 0.25
COURANT = 0.4
RADIX = 8
SLAB = ("ta", "core")
SPACE = ("zh", "zl")
GROUP = ("core", "zl")
EVERY = ("ta", "core", "zh", "zl")


def split_pair(values):
    high = values.astype(jnp.bfloat16)
    return high, (values - high.astype(jnp.float32)).astype(jnp.bfloat16)


def table_pair(values):
    high = lax.reduce_precision(values, 8, 7)
    return jnp.stack([high, values - high]).astype(jnp.bfloat16)


def dot3(left, right):
    def one(a, b):
        return jnp.dot(a, b, preferred_element_type=jnp.float32)

    return one(left[0], right[0]) + (one(left[0], right[1]) + one(left[1], right[0]))


def small_fft(parts, sign):
    count = len(parts)
    if count == 1:
        return parts
    even = small_fft(parts[0::2], sign)
    odd = small_fft(parts[1::2], sign)
    low, high = [], []
    for k in range(count // 2):
        re, im = odd[k]
        if k == 0:
            tr, ti = re, im
        elif 4 * k == count:
            tr, ti = (-im, re) if sign > 0 else (im, -re)
        else:
            c = math.cos(2.0 * math.pi * k / count)
            s = sign * math.sin(2.0 * math.pi * k / count)
            tr, ti = re * c - im * s, re * s + im * c
        low.append((even[k][0] + tr, even[k][1] + ti))
        high.append((even[k][0] - tr, even[k][1] - ti))
    return low + high


def lane_tables(grid_size, sign):
    lanes = grid_size // RADIX
    n = np.arange(lanes)
    angle = 2.0 * np.pi * (n[:, None] * n[None, :] % lanes) / lanes
    c, s = np.cos(angle), sign * np.sin(angle)
    full = jnp.asarray(np.block([[c, s], [-s, c]]), jnp.float32)
    turn = 2.0 * np.pi * (np.arange(RADIX)[:, None] * n[None, :]) / grid_size
    twiddle = np.stack([np.cos(turn), sign * np.sin(turn)]).astype(np.float32)
    return table_pair(full), jnp.asarray(twiddle)


def prop_factors(steps, wave_x, wave_y, grid_size):
    time_step = COURANT / grid_size
    squared = wave_x * wave_x + wave_y * wave_y
    frequency = jnp.sqrt(CORIOLIS * CORIOLIS + squared)
    ratio = squared / (0.25 * grid_size * grid_size)
    log_damp = -HYPERDIFFUSION * (ratio * ratio) * (ratio * ratio)
    phase_angle = frequency * (steps * time_step)
    first_coef = jnp.sin(phase_angle) / frequency
    second_coef = (1.0 - jnp.cos(phase_angle)) / (frequency * frequency)
    damping = jnp.exp(steps * log_damp)
    return jnp.stack([first_coef, second_coef, damping])


def apply_parts(state, factors, kx, ky):
    first, second, damp = factors
    (xr, xi), (yr, yi), (hr, hi) = state
    done = []
    for x, y, p in ((xr, yr, -hi), (xi, yi, hr)):
        m1 = CORIOLIS * y - kx * p
        m2 = -CORIOLIS * x - ky * p
        m3 = kx * x + ky * y
        n1 = CORIOLIS * m2 - kx * m3
        n2 = -CORIOLIS * m1 - ky * m3
        n3 = kx * m1 + ky * m2
        done.append(
            (
                (x + first * m1 + second * n1) * damp,
                (y + first * m2 + second * n2) * damp,
                (p + first * m3 + second * n3) * damp,
            )
        )
    real, imag = done
    return ((real[0], imag[0]), (real[1], imag[1]), (imag[2], -real[2]))


def inverse_kernel(state_ref, kx_ref, ky_ref, mat_ref, tw_ref, out_ref):
    kx, ky = kx_ref[...], ky_ref[...]
    lanes = mat_ref.shape[1] // 2
    chunk = out_ref.shape[4]
    rows = ky.shape[0]
    matrix = (mat_ref[0], mat_ref[1])
    for f in range(4):
        if f < 3:
            re, im = state_ref[f, 0], state_ref[f, 1]
        else:
            re = ky * state_ref[0, 1] - kx * state_ref[1, 1]
            im = kx * state_ref[1, 0] - ky * state_ref[0, 0]
        parts = [
            (re[:, n * lanes : (n + 1) * lanes], im[:, n * lanes : (n + 1) * lanes])
            for n in range(RADIX)
        ]
        parts = small_fft(parts, 1.0)
        turned = []
        for k, (a, b) in enumerate(parts):
            if k > 0:
                c, s = tw_ref[0, k : k + 1], tw_ref[1, k : k + 1]
                a, b = a * c - b * s, a * s + b * c
            turned.append(jnp.concatenate([a, b], axis=1))
        made = dot3(split_pair(jnp.concatenate(turned, axis=0)), matrix)
        for k in range(RADIX):
            for c in range(2):
                block = made[k * rows : (k + 1) * rows, c * lanes : (c + 1) * lanes]
                if chunk >= lanes:
                    g, at = divmod(k * lanes, chunk)
                    out_ref[g, f, c, :, at : at + lanes] = block
                else:
                    per = lanes // chunk
                    for i in range(per):
                        out_ref[k * per + i, f, c] = block[:, i * chunk : (i + 1) * chunk]


def inverse_x(state, tables):
    _, _, rows, grid_size = state.shape
    group = tables["group"]
    chunk = grid_size // group
    step = min(rows, 32)
    mat, tw = tables["inv_x"]
    return pl.pallas_call(
        inverse_kernel,
        grid=(rows // step,),
        in_specs=[
            pl.BlockSpec((3, 2, step, grid_size), lambda i: (0, 0, i, 0)),
            pl.BlockSpec((1, grid_size), lambda i: (0, 0)),
            pl.BlockSpec((step, 1), lambda i: (i, 0)),
            pl.BlockSpec(mat.shape, lambda i: (0, 0, 0)),
            pl.BlockSpec(tw.shape, lambda i: (0, 0, 0)),
        ],
        out_specs=pl.BlockSpec((group, 4, 2, step, chunk), lambda i: (0, 0, 0, i, 0)),
        out_shape=jax.ShapeDtypeStruct((group, 4, 2, rows, chunk), jnp.float32),
        name="inverse_x",
    )(state, tables["kx"], tables["ky"], mat, tw)


def middle_kernel(data_ref, inv_ref, fwd_ref, out_ref, high, low, total):
    at = pl.program_id(0)
    group, _, _, rows, chunk = data_ref.shape
    kept = out_ref.shape[3]

    @pl.when(at == 0)
    def _():
        for f in range(4):
            a, b = split_pair(data_ref[:, f].reshape(group * 2 * rows, chunk))
            high[f], low[f] = a, b

    u, v, h, z = (
        dot3((inv_ref[0], inv_ref[1]), (high[f], low[f])) for f in range(4)
    )
    products = (z * v, z * u, 0.5 * (u * u + v * v), h * u, h * v)
    for f in range(5):
        term = dot3((fwd_ref[0], fwd_ref[1]), split_pair(products[f]))

        @pl.when(at == 0)
        def _():
            total[f] = term

        @pl.when(at > 0)
        def _():
            total[f] = total[f] + term

    @pl.when(at == pl.num_programs(0) - 1)
    def _():
        for f in range(5):
            out_ref[:, f] = total[f].reshape(group, 2, kept, chunk)


def middle(data, tables):
    group, _, _, rows, chunk = data.shape
    inv, fwd = tables["inv_y"], tables["fwd_y"]
    grid_size = inv.shape[1]
    kept = fwd.shape[1] // (2 * group)
    step = grid_size // 4
    return pl.pallas_call(
        middle_kernel,
        grid=(grid_size // step,),
        in_specs=[
            pl.BlockSpec(data.shape, lambda i: (0, 0, 0, 0, 0)),
            pl.BlockSpec((2, step, inv.shape[2]), lambda i: (0, i, 0)),
            pl.BlockSpec((2, fwd.shape[1], step), lambda i: (0, 0, i)),
        ],
        out_specs=pl.BlockSpec((group, 5, 2, kept, chunk), lambda i: (0, 0, 0, 0, 0)),
        out_shape=jax.ShapeDtypeStruct((group, 5, 2, kept, chunk), jnp.float32),
        scratch_shapes=[
            pltpu.VMEM((4, group * 2 * rows, chunk), jnp.bfloat16),
            pltpu.VMEM((4, group * 2 * rows, chunk), jnp.bfloat16),
            pltpu.VMEM((5, group * 2 * kept, chunk), jnp.float32),
        ],
        compiler_params=pltpu.CompilerParams(vmem_limit_bytes=56 * 1024 * 1024),
        name="middle",
    )(data, inv, fwd)


def forward_kernel(kept_steps, dt, limit, data_ref, state_ref, fac_ref, kx_ref, ky_ref, mat_ref, tw_ref, out_ref):
    kx, ky = kx_ref[...], ky_ref[...]
    group, chunk = data_ref.shape[0], data_ref.shape[4]
    rows = ky.shape[0]
    lanes = mat_ref.shape[1] // 2
    factors = (fac_ref[0], fac_ref[1], fac_ref[2])
    state = tuple((state_ref[f, 0], state_ref[f, 1]) for f in range(3))

    def put(values):
        for f in range(3):
            for c in range(2):
                out_ref[f, c] = values[f][c]

    @pl.when(pl.program_id(0) >= kept_steps)
    def _():
        put(apply_parts(state, factors, kx, ky))

    @pl.when(pl.program_id(0) < kept_steps)
    def _():
        matrix = (mat_ref[0], mat_ref[1])

        def piece(f, c, k):
            if chunk >= lanes:
                g, at = divmod(k * lanes, chunk)
                return data_ref[g, f, c, :, at : at + lanes]
            per = lanes // chunk
            return jnp.concatenate([data_ref[k * per + i, f, c] for i in range(per)], axis=1)

        stacked = jnp.concatenate(
            [
                jnp.concatenate([piece(f, 0, k), piece(f, 1, k)], axis=1)
                for f in range(5)
                for k in range(RADIX)
            ],
            axis=0,
        )
        made = dot3(split_pair(stacked), matrix)
        modes = []
        for f in range(5):
            parts = []
            for k in range(RADIX):
                start = (f * RADIX + k) * rows
                a = made[start : start + rows, :lanes]
                b = made[start : start + rows, lanes:]
                if k > 0:
                    c, s = tw_ref[0, k : k + 1], tw_ref[1, k : k + 1]
                    a, b = a * c - b * s, a * s + b * c
                parts.append((a, b))
            parts = small_fft(parts, -1.0)
            modes.append(
                (
                    jnp.concatenate([p[0] for p in parts], axis=1),
                    jnp.concatenate([p[1] for p in parts], axis=1),
                )
            )
        (ar, ai), (br, bi), (kr, ki), (pr, pi), (qr, qi) = modes
        keep = jnp.where((jnp.abs(kx) <= limit) & (ky <= limit), dt, 0.0)
        (xr, xi), (yr, yi), (hr, hi) = state
        put(
            apply_parts(
                (
                    (xr + keep * (ar + kx * ki), xi + keep * (ai - kx * kr)),
                    (yr + keep * (ky * ki - br), yi - keep * (bi + ky * kr)),
                    (hr + keep * (kx * pi + ky * qi), hi - keep * (kx * pr + ky * qr)),
                ),
                factors,
                kx,
                ky,
            )
        )


def forward_x(data, state, tables):
    group, _, _, kept, chunk = data.shape
    _, _, rows, grid_size = state.shape
    step = 8
    kept_steps = kept // step
    mat, tw = tables["fwd_x"]

    def kernel(*refs):
        forward_kernel(kept_steps, COURANT / grid_size, float(grid_size // 3), *refs)

    return pl.pallas_call(
        kernel,
        grid=(rows // step,),
        in_specs=[
            pl.BlockSpec(
                (group, 5, 2, step, chunk),
                lambda i: (0, 0, 0, jnp.minimum(i, kept_steps - 1), 0),
            ),
            pl.BlockSpec((3, 2, step, grid_size), lambda i: (0, 0, i, 0)),
            pl.BlockSpec((3, step, grid_size), lambda i: (0, i, 0)),
            pl.BlockSpec((1, grid_size), lambda i: (0, 0)),
            pl.BlockSpec((step, 1), lambda i: (i, 0)),
            pl.BlockSpec(mat.shape, lambda i: (0, 0, 0)),
            pl.BlockSpec(tw.shape, lambda i: (0, 0, 0)),
        ],
        out_specs=pl.BlockSpec((3, 2, step, grid_size), lambda i: (0, 0, i, 0)),
        out_shape=jax.ShapeDtypeStruct(state.shape, jnp.float32),
        name="forward_x",
    )(data, state, tables["factors"], tables["kx"], tables["ky"], mat, tw)


def scan_kernel(data_ref, fac_ref, kx_ref, ky_ref, out_ref):
    kx, ky = kx_ref[...], ky_ref[...]
    factors = (fac_ref[0], fac_ref[1], fac_ref[2])
    carried = None
    for k in range(data_ref.shape[0]):
        new = tuple((data_ref[k, f, 0], data_ref[k, f, 1]) for f in range(3))
        if carried is not None:
            moved = apply_parts(carried, factors, kx, ky)
            new = tuple(
                (moved[f][0] + new[f][0], moved[f][1] + new[f][1]) for f in range(3)
            )
        for f in range(3):
            for c in range(2):
                out_ref[k, f, c] = new[f][c]
        carried = new


def slab_scan(data, factors, kx, ky):
    slabs, _, _, rows, grid_size = data.shape
    step = grid_size // 8
    return pl.pallas_call(
        scan_kernel,
        grid=(grid_size // step,),
        in_specs=[
            pl.BlockSpec((slabs, 3, 2, rows, step), lambda i: (0, 0, 0, 0, i)),
            pl.BlockSpec((3, rows, step), lambda i: (0, 0, i)),
            pl.BlockSpec((1, step), lambda i: (0, i)),
            pl.BlockSpec((rows, 1), lambda i: (0, 0)),
        ],
        out_specs=pl.BlockSpec((slabs, 3, 2, rows, step), lambda i: (0, 0, 0, 0, i)),
        out_shape=jax.ShapeDtypeStruct(data.shape, jnp.float32),
        name="slab_scan",
    )(data, factors, kx, ky)


def make_tables(grid_size, rows, group, mine):
    counter = jnp.arange(grid_size, dtype=jnp.int32)
    kx = jnp.where(counter < grid_size // 2, counter, counter - grid_size).astype(jnp.float32)[None]
    ky = (group * jnp.arange(rows, dtype=jnp.int32) + mine).astype(jnp.float32)[:, None]
    kept = -(-(grid_size // 3 + 1) // group)
    kept = min(rows, -(-kept // 8) * 8)
    freq = (
        group * jnp.arange(rows, dtype=jnp.int32)[None]
        + jnp.arange(group, dtype=jnp.int32)[:, None]
    )
    turns = freq[:, :, None] * counter % grid_size
    angle = 2.0 * math.pi / grid_size * turns.astype(jnp.float32)
    waves = jnp.stack([jnp.cos(angle), -jnp.sin(angle)], axis=1)
    forward = (waves[:, :, :kept] / grid_size).reshape(group * 2 * kept, grid_size)
    turns = counter[:, None, None] * freq[None] % grid_size
    angle = 2.0 * math.pi / grid_size * turns.astype(jnp.float32)
    weight = jnp.where(freq == 0, 1.0, 2.0).astype(jnp.float32) / grid_size
    inverse = jnp.stack([weight * jnp.cos(angle), -weight * jnp.sin(angle)], axis=2)
    inverse = inverse.reshape(grid_size, group * 2 * rows)
    return {
        "group": group,
        "kx": kx,
        "ky": ky,
        "inv_y": table_pair(inverse),
        "fwd_y": table_pair(forward),
        "inv_x": lane_tables(grid_size, 1.0),
        "fwd_x": lane_tables(grid_size, -1.0),
        "factors": prop_factors(1.0, kx, ky, grid_size),
    }


def fine_step(state, tables):
    rotated = inverse_x(state, tables)
    rotated = lax.all_to_all(rotated, GROUP, split_axis=0, concat_axis=0, tiled=True)
    partial_y = middle(rotated, tables)
    partial_y = lax.all_to_all(partial_y, GROUP, split_axis=0, concat_axis=0, tiled=True)
    return forward_x(partial_y, state, tables)


def gathered(values, slabs, group, back):
    _, _, rows, grid_size = values.shape
    half = group // 2
    ident = lax.axis_index(SPACE)
    own = lax.axis_index(GROUP)
    per = rows // group
    shift = 0 if back else 1
    if back:
        pieces = values.reshape(3, 2, group, per, grid_size)
    else:
        pieces = values.reshape(3, 2, per, group, grid_size).transpose(3, 0, 1, 2, 4)

    landed = []
    for turn in range(group):
        links = []
        for slab in range(slabs):
            to_slab = (slab + shift) % slabs
            for z in range(group):
                q = (z + turn) % group
                far = (((to_slab // 2) * 2 + q // half) * 2 + to_slab % 2) * half + q % half
                near = slab * group + z
                links.append((far, near) if back else (near, far))
        if back:
            piece = lax.dynamic_index_in_dim(pieces, (own - turn) % group, 2, keepdims=False)
        else:
            piece = lax.dynamic_index_in_dim(pieces, (ident + turn) % group, 0, keepdims=False)
        landed.append(lax.ppermute(piece, EVERY, links))
    stacked = jnp.stack(landed)
    order = jnp.arange(group, dtype=jnp.int32)
    if back:
        stacked = jnp.take(stacked, (order - ident) % group, axis=0)
        return stacked.transpose(1, 2, 3, 0, 4).reshape(values.shape)
    stacked = jnp.take(stacked, (own - order) % group, axis=0)
    return stacked.transpose(1, 2, 0, 3, 4).reshape(values.shape)


def shards(c_state, init):
    rows, grid_size = c_state.shape[3:]
    group = lax.axis_size(SPACE)
    slabs = lax.axis_size(SLAB)
    own_slab = lax.axis_index(SLAB)
    tables = make_tables(grid_size, rows, group, lax.axis_index(GROUP))
    current = c_state[0]
    current = gathered(jnp.where(own_slab == slabs - 1, init, current), slabs, group, False)
    for _ in range(CF):
        current = fine_step(current, tables)
    residual = gathered(current, slabs, group, True) - c_state[0]

    per = rows // slabs
    start = lax.axis_index(SPACE) * rows + own_slab * per
    ky = (start + jnp.arange(per, dtype=jnp.int32)).astype(jnp.float32)[:, None]
    coarse = prop_factors(float(CF), tables["kx"], ky, grid_size)
    split = residual.reshape(3, 2, slabs, per, grid_size).transpose(2, 0, 1, 3, 4)
    split = lax.all_to_all(split, SLAB, split_axis=0, concat_axis=0, tiled=True)
    split = slab_scan(split, coarse, tables["kx"], ky)
    split = lax.all_to_all(split, SLAB, split_axis=0, concat_axis=0, tiled=True)
    moved = split.transpose(1, 2, 0, 3, 4).reshape(residual.shape)
    return (c_state + moved[None], residual[None])


def solution(mesh):
    slabs, space = mesh.devices.shape
    fine = Mesh(mesh.devices.reshape(slabs // 2, 2, 2, space // 2), EVERY)
    spec = P(SLAB, None, None, SPACE, None)
    return jax.shard_map(
        shards,
        mesh=fine,
        in_specs=(spec, P(None, None, SPACE, None)),
        out_specs=(spec, spec),
        check_vma=False,
    )
```

time: 970 us -> 580 us (0.60)
  waiting for transfers between devices: 397 us -> 260 us
  matrix products: 113 us -> 0 us
  other arithmetic: 154 us -> 51.5 us
  Pallas kernels: 0 us -> 99.7 us
  blocking collectives: 141 us -> 54 us
  local copies, waits for them, and re-layouts: 104 us -> 42.7 us
  starting transfers between devices: 20 us -> 63.5 us
  loops' own time: 15.2 us -> 0 us
  between operations: 15.3 us -> 1.3 us
    all_to_all x3 -> x5, waiting for transfers between devices: 292 us -> 159 us  [the longest x2 80.2 us: fine_step(): lax.all_to_all(partial_y, GROUP, split_axis=0, concat_axis=0, tiled=True)]
    dot_general x12 -> x0, matrix products: 113 us -> none  [the longest x2 34 us: fine_step(): jnp.einsum('fxy,cly->fclx', products, tables['forward_y'], precision=PREC...]
    all_gather x1 -> x0, waiting for transfers between devices: 105 us -> none  [entering(): pieces = jax.tree.map(lambda part: lax.all_gather(part, axis), value)]
    ppermute x1 -> x8, waiting for transfers between devices: 0.01 us -> 101 us  [gathered(): landed.append(lax.ppermute(piece, EVERY, links))]
    pallas_call x0 -> x7, Pallas kernels: none -> 99.7 us  [the longest x2 53.9 us: middle(): pl.pallas_call(middle_kernel, grid=(grid_size // step,), in_specs=[pl.Blo...]
    unnamed x1 -> x0, blocking collectives: 44 us -> none
    all_to_all x1, blocking collectives: 97 us -> 54 us  [fine_step(): lax.all_to_all(rotated, GROUP, split_axis=0, concat_axis=0, tiled=True)]
    mul x25 -> x2, other arithmetic: 41.3 us -> 8.26 us  [the longest x1 8.26 us: make_tables(): weight * jnp.cos(angle)]
  transfers between devices with their start and end apart: 5 -> 13, of which waited for: 4 -> 10; matrix products, arithmetic and copies ran while one was open for 4% -> 9% of each run, Pallas kernels for 0% -> 0%
where the time goes in v1:
time: 580 us; the launch traced here: 572 us
  waiting for transfers between devices  260 us (45%)
  Pallas kernels  99.7 us (17%)
  starting transfers between devices  63.5 us (11%)
  blocking collectives  54 us (9%)
  other arithmetic  51.5 us (9%)
  local copies, waits for them, and re-layouts  42.7 us (7%)
    ppermute x8, waiting for transfers between devices, gathered(): landed.append(lax.ppermute(piece, EVERY, links))  101 us
    all_to_all x2, waiting for transfers between devices, fine_step(): lax.all_to_all(partial_y, GROUP, split_axis=0, concat_axis=0, tiled=True)  80.2 us
    all_to_all x2, waiting for transfers between devices, shards(): split = lax.all_to_all(split, SLAB, split_axis=0, concat_axis=0, tiled=True)  66.9 us
    all_to_all x1, blocking collectives, fine_step(): lax.all_to_all(rotated, GROUP, split_axis=0, concat_axis=0, tiled=True)  54 us
    pallas_call x2, Pallas kernels, middle(): pl.pallas_call(middle_kernel, grid=(grid_size // step,), in_specs=[pl.Blo...  53.9 us
    pallas_call x2, Pallas kernels, forward_x(): pl.pallas_call(kernel, grid=(rows // step,), in_specs=[pl.BlockSpec((grou...  27.1 us
    all_to_all x2, starting transfers between devices, shards(): split = lax.all_to_all(split, SLAB, split_axis=0, concat_axis=0, tiled=True)  25.5 us
    ppermute x8, starting transfers between devices, gathered(): landed.append(lax.ppermute(piece, EVERY, links))  18.4 us
  transfers between devices with their start and end apart: 13, of which 10 were waited for; matrix products, arithmetic and copies ran while one was open for 9% of the time, Pallas kernels for 0%

profile of v1, /device:TPU:0, one launch (start us, length us, event | category | flops | bytes accessed | tf_op | source)
XLA Modules:
  0.0 572.5 jit_solution(14761035918973262679)
XLA Ops:
  0.7 4.5 bitcast_select_fusion
  5.2 3.1 reshape.672
  8.3 3.3 constant_dynamic-slice_fusion.3
  12.8 4.1 collective-permute-start
  19.9 3.2 collective-permute-start.2
  24.1 2.3 collective-permute-start.3
  27.7 33.0 %collective-permute-done = f32[3,2,32,1024]{3,2,1,0:T(8,128)S(1)} collective-permute-done((f32[3,2,32,1024]{3,2,1,0:T(8,128)}, f32[3,2,32,1024]{3,2,1,0:T(8,128)S(1)}, u32[]{:S(2)}, u32[]{:S(2)}) %collective-permute-start) | collective-permute-done | bytes 786464 | tf_op jit(solution)/shard_map/ppermute | solution.py:426
  60.7 21.1 %collective-permute-done.2 = f32[3,2,32,1024]{3,2,1,0:T(8,128)S(1)} collective-permute-done((f32[3,2,32,1024]{3,2,1,0:T(8,128)}, f32[3,2,32,1024]{3,2,1,0:T(8,128)S(1)}, u32[]{:S(2)}, u32[]{:S(2)}) %collective-permute-start.2) | collective-permute-done | bytes 786464 | tf_op jit(solution)/shard_map/ppermute | solution.py:426
  84.9 2.4 gather_fusion
  87.4 2.3 select_bitcast_fusion.1
  91.6 5.9 %inverse_x.2 = f32[4,4,2,128,256]{4,3,2,1,0:T(8,128)} custom-call(f32[3,2,128,1024]{3,2,1,0:T(8,128)} %bitcast.47, f32[1,1024]{1,0:T(1,128)} %fusion.40.kx_ref.refs_3_, f32[128,1]{1,0:T(8,128)} %add_convert_fusion.ky_ref.refs_4_, bf16[2,256,256]{2,1,0:T(8,128)(2,1)} %constant.191.mat_ref, f32[2,8,128]{2,1,0:T(8,128)} %constant.181.clone.tw_ref), custom_call_target="tpu_custom_call" | custom-call | tf_op jit(solution)/shard_map/inverse_x/pallas_call | solution.py:149
  97.5 10.1 %all-to-all-start = ((f32[4,4,2,128,256]{4,3,2,1,0:T(8,128)}), f32[4,4,2,128,256]{4,3,2,1,0:T(8,128)}, u32[]{:S(2)}, u32[]{:S(2)}) async-start(f32[4,4,2,128,256]{4,3,2,1,0:T(8,128)} %inverse_x.2), calls=%async_computation | async-start | bytes 8388608 | tf_op jit(solution)/shard_map/all_to_all | solution.py:394
  107.7 8.3 %cosine_multiply_fusion = (f32[1024,4,1,128]{3,0,2,1:T(8,128)S(1)}, f32[1024,4,1,128]{3,0,2,1:T(8,128)S(1)}) fusion(s32[4,128]{1,0:T(4,128)S(1)} %iota_add_fusion, f32[4,128]{1,0:T(4,128)S(1)} %get-tuple-element.29, f32[4,128]{1,0:T(4,128)S(1)} %get-tuple-element.30), kind=kLoop, calls=%fused_computation.37 | loop fusion | flops 8388608 | bytes 4200448 | tf_op jit(solution)/shard_map/mul | solution.py:378
  116.2 5.4 copy.34
  121.6 6.4 %reshape.674 = f32[1,1024,1024]{2,1,0:T(8,128)} reshape(f32[1024,4,2,128]{3,2,1,0:T(2,128)} %copy.34) | data formatting | bytes 8388608 | tf_op jit(solution)/shard_map/reshape | solution.py:379
  128.0 8.3 %fusion.16 = (f32[4,1,128,1024]{3,2,1,0:T(8,128)S(1)}, f32[4,1,128,1024]{3,2,1,0:T(8,128)S(1)}) fusion(s32[4,128]{1,0:T(4,128)S(1)} %iota_add_fusion), kind=kLoop, calls=%fused_computation.43 | loop fusion | flops 7864320 | bytes 4196352 | tf_op jit(solution)/shard_map/cos | solution.py:373
  141.6 2.3 pad_maximum_fusion.1.inv_ref
  143.9 11.8 %all-to-all-done.data_ref = f32[4,4,2,128,256]{4,3,2,1,0:T(8,128)} async-done(((f32[4,4,2,128,256]{4,3,2,1,0:T(8,128)}), f32[4,4,2,128,256]{4,3,2,1,0:T(8,128)}, u32[]{:S(2)}, u32[]{:S(2)}) %all-to-all-start) | async-done | bytes 4194336 | tf_op jit(solution)/shard_map/all_to_all | solution.py:394
  155.7 27.1 %middle.2 = f32[4,5,2,88,256]{4,3,2,1,0:T(8,128)} custom-call(f32[4,4,2,128,256]{4,3,2,1,0:T(8,128)} %all-to-all-done.data_ref, bf16[2,1024,1024]{2,1,0:T(8,128)(2,1)} %pad_maximum_fusion.1.inv_ref, bf16[2,704,1024]{2,1,0:T(8,128)(2,1)} %pad_maximum_fusion.5.fwd_ref), custom_call_target="tpu_custom_call" | custom-call | tf_op jit(solution)/shard_map/middle/pallas_call | solution.py:203
  182.9 4.8 all-to-all-start.1
  187.7 2.2 fusion.19
  191.2 38.4 %all-to-all-done.1.refs_0_ = f32[4,5,2,88,256]{4,3,2,1,0:T(8,128)} async-done(((f32[4,5,2,88,256]{4,3,2,1,0:T(8,128)}), f32[4,5,2,88,256]{4,3,2,1,0:T(8,128)}, u32[]{:S(2)}, u32[]{:S(2)}) %all-to-all-start.1) | async-done | bytes 3604512 | tf_op jit(solution)/shard_map/all_to_all | solution.py:396
  229.5 13.5 %forward_x.2.state_ref.refs_1_ = f32[3,2,128,1024]{3,2,1,0:T(8,128)} custom-call(f32[4,5,2,88,256]{4,3,2,1,0:T(8,128)} %all-to-all-done.1.refs_0_, f32[3,2,128,1024]{3,2,1,0:T(8,128)} %bitcast.48, f32[3,128,1024]{2,1,0:T(8,128)} %pad_maximum_fusion.6.refs_2_, f32[1,1024]{1,0:T(1,128)} %fusion.40.kx_ref.refs_3_, f32[128,1]{1,0:T(8,128)} %add_convert_fusion.ky_ref.refs_4_, ...), custom_call_target="tpu_custom_call" | custom-call | tf_op jit(solution)/shard_map/forward_x/pallas_call | solution.py:305
  243.1 6.0 %inverse_x.3 = f32[4,4,2,128,256]{4,3,2,1,0:T(8,128)} custom-call(f32[3,2,128,1024]{3,2,1,0:T(8,128)} %forward_x.2.state_ref.refs_1_, f32[1,1024]{1,0:T(1,128)} %fusion.40.kx_ref.refs_3_, f32[128,1]{1,0:T(8,128)} %add_convert_fusion.ky_ref.refs_4_, bf16[2,256,256]{2,1,0:T(8,128)(2,1)} %constant.191.mat_ref, f32[2,8,128]{2,1,0:T(8,128)} %constant.181.clone.tw_ref), custom_call_target="tpu_custom_call" | custom-call | tf_op jit(solution)/shard_map/inverse_x/pallas_call | solution.py:149
  249.0 54.0 %all_to_all.30.data_ref = f32[4,4,2,128,256]{4,3,2,1,0:T(8,128)} all-to-all(f32[4,4,2,128,256]{4,3,2,1,0:T(8,128)} %inverse_x.3), channel_id=1, replica_groups=mesh['ta'=4,'core'=2,'zh'=2,'zl'=2] {'core','zl'}, dimensions={0} | all-to-all | bytes 8388608 | tf_op jit(solution)/shard_map/all_to_all | solution.py:394
  303.0 26.8 %middle.3 = f32[4,5,2,88,256]{4,3,2,1,0:T(8,128)} custom-call(f32[4,4,2,128,256]{4,3,2,1,0:T(8,128)} %all_to_all.30.data_ref, bf16[2,1024,1024]{2,1,0:T(8,128)(2,1)} %pad_maximum_fusion.1.inv_ref, bf16[2,704,1024]{2,1,0:T(8,128)(2,1)} %pad_maximum_fusion.5.fwd_ref), custom_call_target="tpu_custom_call" | custom-call | tf_op jit(solution)/shard_map/middle/pallas_call | solution.py:203
  329.8 4.7 all-to-all-start.3
  334.6 41.8 %all-to-all-done.3.refs_0_ = f32[4,5,2,88,256]{4,3,2,1,0:T(8,128)} async-done(((f32[4,5,2,88,256]{4,3,2,1,0:T(8,128)}), f32[4,5,2,88,256]{4,3,2,1,0:T(8,128)}, u32[]{:S(2)}, u32[]{:S(2)}) %all-to-all-start.3) | async-done | bytes 3604512 | tf_op jit(solution)/shard_map/all_to_all | solution.py:396
  376.4 13.5 %forward_x.3 = f32[3,2,128,1024]{3,2,1,0:T(8,128)} custom-call(f32[4,5,2,88,256]{4,3,2,1,0:T(8,128)} %all-to-all-done.3.refs_0_, f32[3,2,128,1024]{3,2,1,0:T(8,128)} %forward_x.2.state_ref.refs_1_, f32[3,128,1024]{2,1,0:T(8,128)} %pad_maximum_fusion.6.refs_2_, f32[1,1024]{1,0:T(1,128)} %fusion.40.kx_ref.refs_3_, f32[128,1]{1,0:T(8,128)} %add_convert_fusion.ky_ref.refs_4_, ...), custom_call_target="tpu_custom_call" | custom-call | tf_op jit(solution)/shard_map/forward_x/pallas_call | solution.py:305
  389.9 2.1 dynamic-slice_bitcast_fusion.3
  392.7 3.5 collective-permute-start.5
  396.3 3.6 collective-permute-start.7
  400.0 14.9 %collective-permute-done.5 = f32[3,2,32,1024]{3,2,1,0:T(8,128)S(1)} collective-permute-done((f32[3,2,32,1024]{3,2,1,0:T(8,128)S(1)}, f32[3,2,32,1024]{3,2,1,0:T(8,128)S(1)}, u32[]{:S(2)}, u32[]{:S(2)}) %collective-permute-start.5) | collective-permute-done | bytes 786464 | tf_op jit(solution)/shard_map/ppermute | solution.py:426
  414.9 16.2 %collective-permute-done.6 = f32[3,2,32,1024]{3,2,1,0:T(8,128)S(1)} collective-permute-done((f32[3,2,32,1024]{3,2,1,0:T(8,128)S(1)}, f32[3,2,32,1024]{3,2,1,0:T(8,128)S(1)}, u32[]{:S(2)}, u32[]{:S(2)}) %collective-permute-start.6) | collective-permute-done | bytes 786464 | tf_op jit(solution)/shard_map/ppermute | solution.py:426
  431.0 15.8 %collective-permute-done.7 = f32[3,2,32,1024]{3,2,1,0:T(8,128)S(1)} collective-permute-done((f32[3,2,32,1024]{3,2,1,0:T(8,128)S(1)}, f32[3,2,32,1024]{3,2,1,0:T(8,128)S(1)}, u32[]{:S(2)}, u32[]{:S(2)}) %collective-permute-start.7) | collective-permute-done | bytes 786464 | tf_op jit(solution)/shard_map/ppermute | solution.py:426
  447.1 2.4 gather_fusion.1
  449.5 2.3 select_bitcast_fusion
  451.8 2.4 copy.35
  455.9 3.2 fusion.1
  459.0 20.8 %all-to-all-start.4 = ((f32[8,3,2,16,1024]{4,3,2,1,0:T(8,128)}), f32[8,3,2,16,1024]{4,3,2,1,0:T(8,128)}, u32[]{:S(2)}, u32[]{:S(2)}) async-start(f32[8,3,2,16,1024]{4,3,2,1,0:T(8,128)} %fusion.1), calls=%async_computation.4 | async-start | bytes 6291456 | tf_op jit(solution)/shard_map/all_to_all | solution.py:453
  481.5 36.7 %all-to-all-done.4.data_ref = f32[8,3,2,16,1024]{4,3,2,1,0:T(8,128)} async-done(((f32[8,3,2,16,1024]{4,3,2,1,0:T(8,128)}), f32[8,3,2,16,1024]{4,3,2,1,0:T(8,128)}, u32[]{:S(2)}, u32[]{:S(2)}) %all-to-all-start.4) | async-done | bytes 3145760 | tf_op jit(solution)/shard_map/all_to_all | solution.py:453
  518.2 6.8 %slab_scan.1 = f32[8,3,2,16,1024]{4,3,2,1,0:T(8,128)} custom-call(f32[8,3,2,16,1024]{4,3,2,1,0:T(8,128)} %all-to-all-done.4.data_ref, f32[3,16,1024]{2,1,0:T(8,128)} %pad_maximum_fusion.7.fac_ref, f32[1,1024]{1,0:T(1,128)} %fusion.40.kx_ref.refs_3_, f32[16,1]{1,0:T(8,128)} %add_convert_fusion.1.ky_ref), custom_call_target="tpu_custom_call" | custom-call | tf_op jit(solution)/shard_map/slab_scan/pallas_call | solution.py:346
  525.1 4.7 all-to-all-start.5
  529.8 5.1 copy_subtract_fusion
  534.9 2.6 copy.41
  537.5 30.2 %all-to-all-done.5 = f32[8,3,2,16,1024]{4,3,2,1,0:T(8,128)} async-done(((f32[8,3,2,16,1024]{4,3,2,1,0:T(8,128)}), f32[8,3,2,16,1024]{4,3,2,1,0:T(8,128)}, u32[]{:S(2)}, u32[]{:S(2)}) %all-to-all-start.5) | async-done | bytes 3145760 | tf_op jit(solution)/shard_map/all_to_all | solution.py:455
  567.6 2.3 copy.38
  569.9 2.3 add.359
  (50 shorter events, 22.5 us)
Async XLA Ops:
  12.8 47.9 %collective-permute-start = (f32[3,2,32,1024]{3,2,1,0:T(8,128)}, f32[3,2,32,1024]{3,2,1,0:T(8,128)S(1)}, u32[]{:S(2)}, u32[]{:S(2)}) collective-permute-start(f32[3,2,32,1024]{3,2,1,0:T(8,128)} %bitcast.45), channel_id=1, source_target_pairs={{0,2},{1,3},{2,6},{3,7},{4,8},{5,9},{6,12},{7,13},{8,10},{9,11},{1... | collective-permute-start | bytes 2359304 | tf_op jit(solution)/shard_map/ppermute | solution.py:426
  17.9 42.8 %collective-permute-start.1 = (f32[3,2,32,1024]{3,2,1,0:T(8,128)}, f32[3,2,32,1024]{3,2,1,0:T(8,128)S(1)}, u32[]{:S(2)}, u32[]{:S(2)}) collective-permute-start(f32[3,2,32,1024]{3,2,1,0:T(8,128)} %bitcast.44), channel_id=1, source_target_pairs={{0,3},{1,6},{2,7},{3,2},{4,9},{5,12},{6,13},{7,8},{8,11},{9,14},{1... | collective-permute-start | bytes 2359304 | tf_op jit(solution)/shard_map/ppermute | solution.py:426
  19.9 61.8 %collective-permute-start.2 = (f32[3,2,32,1024]{3,2,1,0:T(8,128)}, f32[3,2,32,1024]{3,2,1,0:T(8,128)S(1)}, u32[]{:S(2)}, u32[]{:S(2)}) collective-permute-start(f32[3,2,32,1024]{3,2,1,0:T(8,128)} %bitcast.43), channel_id=1, source_target_pairs={{0,6},{1,7},{2,2},{3,3},{4,12},{5,13},{6,8},{7,9},{8,14},{9,15},{1... | collective-permute-start | bytes 2359304 | tf_op jit(solution)/shard_map/ppermute | solution.py:426
  24.1 57.6 %collective-permute-start.3 = (f32[3,2,32,1024]{3,2,1,0:T(8,128)}, f32[3,2,32,1024]{3,2,1,0:T(8,128)S(1)}, u32[]{:S(2)}, u32[]{:S(2)}) collective-permute-start(f32[3,2,32,1024]{3,2,1,0:T(8,128)} %bitcast.42), channel_id=1, source_target_pairs={{0,7},{1,2},{2,3},{3,6},{4,13},{5,8},{6,9},{7,12},{8,15},{9,10},{1... | collective-permute-start | bytes 2359304 | tf_op jit(solution)/shard_map/ppermute | solution.py:426
  60.7 21.1 %copy-start.3 = (f32[3,2,32,1024]{3,2,1,0:T(8,128)}, f32[3,2,32,1024]{3,2,1,0:T(8,128)S(1)}, u32[]{:S(2)}) copy-start(f32[3,2,32,1024]{3,2,1,0:T(8,128)S(1)} %collective-permute-done) | copy-start | bytes 2359300
  60.7 21.1 %copy-start.4 = (f32[3,2,32,1024]{3,2,1,0:T(8,128)}, f32[3,2,32,1024]{3,2,1,0:T(8,128)S(1)}, u32[]{:S(2)}) copy-start(f32[3,2,32,1024]{3,2,1,0:T(8,128)S(1)} %collective-permute-done.1) | copy-start | bytes 2359300
  81.7 0.9 copy-start.5
  81.7 1.1 copy-start.6
  97.5 58.2 %all-to-all-start = ((f32[4,4,2,128,256]{4,3,2,1,0:T(8,128)}), f32[4,4,2,128,256]{4,3,2,1,0:T(8,128)}, u32[]{:S(2)}, u32[]{:S(2)}) async-start(f32[4,4,2,128,256]{4,3,2,1,0:T(8,128)} %inverse_x.2), calls=%async_computation | async-start | bytes 8388608 | tf_op jit(solution)/shard_map/all_to_all | solution.py:394
  137.4 3.2 copy-start.2
  182.9 46.7 %all-to-all-start.1 = ((f32[4,5,2,88,256]{4,3,2,1,0:T(8,128)}), f32[4,5,2,88,256]{4,3,2,1,0:T(8,128)}, u32[]{:S(2)}, u32[]{:S(2)}) async-start(f32[4,5,2,88,256]{4,3,2,1,0:T(8,128)} %middle.2), calls=%async_computation.1 | async-start | bytes 7208960 | tf_op jit(solution)/shard_map/all_to_all | solution.py:396
  329.8 46.6 %all-to-all-start.3 = ((f32[4,5,2,88,256]{4,3,2,1,0:T(8,128)}), f32[4,5,2,88,256]{4,3,2,1,0:T(8,128)}, u32[]{:S(2)}, u32[]{:S(2)}) async-start(f32[4,5,2,88,256]{4,3,2,1,0:T(8,128)} %middle.3), calls=%async_computation.3 | async-start | bytes 7208960 | tf_op jit(solution)/shard_map/all_to_all | solution.py:396
  392.0 7.9 %collective-permute-start.4 = (f32[3,2,32,1024]{3,2,1,0:T(8,128)S(1)}, f32[3,2,32,1024]{3,2,1,0:T(8,128)S(1)}, u32[]{:S(2)}, u32[]{:S(2)}) collective-permute-start(f32[3,2,32,1024]{3,2,1,0:T(8,128)S(1)} %get-tuple-element.9), channel_id=1, source_target_pairs={{0,0},{1,1},{4,2},{5,3},{2,4},{3,5},{6,6},{7,7},{8,8},{9,9},{12,10... | collective-permute-start | bytes 2359304 | tf_op jit(solution)/shard_map/ppermute | solution.py:426
  392.7 22.1 %collective-permute-start.5 = (f32[3,2,32,1024]{3,2,1,0:T(8,128)S(1)}, f32[3,2,32,1024]{3,2,1,0:T(8,128)S(1)}, u32[]{:S(2)}, u32[]{:S(2)}) collective-permute-start(f32[3,2,32,1024]{3,2,1,0:T(8,128)S(1)} %get-tuple-element.12), channel_id=1, source_target_pairs={{1,0},{4,1},{5,2},{0,3},{3,4},{6,5},{7,6},{2,7},{9,8},{12,9},{13,1... | collective-permute-start | bytes 2359304 | tf_op jit(solution)/shard_map/ppermute | solution.py:426
  396.3 34.8 %collective-permute-start.6 = (f32[3,2,32,1024]{3,2,1,0:T(8,128)S(1)}, f32[3,2,32,1024]{3,2,1,0:T(8,128)S(1)}, u32[]{:S(2)}, u32[]{:S(2)}) collective-permute-start(f32[3,2,32,1024]{3,2,1,0:T(8,128)S(1)} %get-tuple-element.11), channel_id=1, source_target_pairs={{4,0},{5,1},{0,2},{1,3},{6,4},{7,5},{2,6},{3,7},{12,8},{13,9},{8,1... | collective-permute-start | bytes 2359304 | tf_op jit(solution)/shard_map/ppermute | solution.py:426
  396.3 50.6 %collective-permute-start.7 = (f32[3,2,32,1024]{3,2,1,0:T(8,128)S(1)}, f32[3,2,32,1024]{3,2,1,0:T(8,128)S(1)}, u32[]{:S(2)}, u32[]{:S(2)}) collective-permute-start(f32[3,2,32,1024]{3,2,1,0:T(8,128)S(1)} %get-tuple-element.10), channel_id=1, source_target_pairs={{5,0},{0,1},{1,2},{4,3},{7,4},{2,5},{3,6},{6,7},{13,8},{8,9},{9,10... | collective-permute-start | bytes 2359304 | tf_op jit(solution)/shard_map/ppermute | solution.py:426
  451.8 4.1 copy-start
  454.2 1.6 copy-start.1
  459.0 59.2 %all-to-all-start.4 = ((f32[8,3,2,16,1024]{4,3,2,1,0:T(8,128)}), f32[8,3,2,16,1024]{4,3,2,1,0:T(8,128)}, u32[]{:S(2)}, u32[]{:S(2)}) async-start(f32[8,3,2,16,1024]{4,3,2,1,0:T(8,128)} %fusion.1), calls=%async_computation.4 | async-start | bytes 6291456 | tf_op jit(solution)/shard_map/all_to_all | solution.py:453
  525.1 42.5 %all-to-all-start.5 = ((f32[8,3,2,16,1024]{4,3,2,1,0:T(8,128)}), f32[8,3,2,16,1024]{4,3,2,1,0:T(8,128)}, u32[]{:S(2)}, u32[]{:S(2)}) async-start(f32[8,3,2,16,1024]{4,3,2,1,0:T(8,128)} %slab_scan.1), calls=%async_computation.5 | async-start | bytes 6291456 | tf_op jit(solution)/shard_map/all_to_all | solution.py:455

commit v2 on v1

--- a/solution.py
+++ b/solution.py
@@ -13,6 +13,7 @@
 HYPERDIFFUSION = 0.25
 COURANT = 0.4
 RADIX = 8
+STREAMS = 2
 SLAB = ("ta", "core")
 SPACE = ("zh", "zl")
 GROUP = ("core", "zl")
@@ -104,10 +105,11 @@
     return ((real[0], imag[0]), (real[1], imag[1]), (imag[2], -real[2]))
 
 
-def inverse_kernel(state_ref, kx_ref, ky_ref, mat_ref, tw_ref, out_ref):
+def inverse_kernel(state_ref, kx_ref, ky_ref, mat_ref, tw_ref, *outs):
     kx, ky = kx_ref[...], ky_ref[...]
     lanes = mat_ref.shape[1] // 2
-    chunk = out_ref.shape[4]
+    width = outs[0].shape[4]
+    chunk = width * len(outs)
     rows = ky.shape[0]
     matrix = (mat_ref[0], mat_ref[1])
     for f in range(4):
@@ -133,17 +135,21 @@
                 block = made[k * rows : (k + 1) * rows, c * lanes : (c + 1) * lanes]
                 if chunk >= lanes:
                     g, at = divmod(k * lanes, chunk)
-                    out_ref[g, f, c, :, at : at + lanes] = block
+                    o, at = divmod(at, width)
+                    outs[o][g, f, c, :, at : at + lanes] = block
                 else:
                     per = lanes // chunk
                     for i in range(per):
-                        out_ref[k * per + i, f, c] = block[:, i * chunk : (i + 1) * chunk]
+                        outs[0][k * per + i, f, c] = block[:, i * chunk : (i + 1) * chunk]
 
 
 def inverse_x(state, tables):
     _, _, rows, grid_size = state.shape
     group = tables["group"]
     chunk = grid_size // group
+    lanes = grid_size // RADIX
+    count = 2 if chunk % (2 * lanes) == 0 else 1
+    width = chunk // count
     step = min(rows, 32)
     mat, tw = tables["inv_x"]
     return pl.pallas_call(
@@ -156,8 +162,8 @@
             pl.BlockSpec(mat.shape, lambda i: (0, 0, 0)),
             pl.BlockSpec(tw.shape, lambda i: (0, 0, 0)),
         ],
-        out_specs=pl.BlockSpec((group, 4, 2, step, chunk), lambda i: (0, 0, 0, i, 0)),
-        out_shape=jax.ShapeDtypeStruct((group, 4, 2, rows, chunk), jnp.float32),
+        out_specs=[pl.BlockSpec((group, 4, 2, step, width), lambda i: (0, 0, 0, i, 0))] * count,
+        out_shape=[jax.ShapeDtypeStruct((group, 4, 2, rows, width), jnp.float32)] * count,
         name="inverse_x",
     )(state, tables["kx"], tables["ky"], mat, tw)
 
@@ -171,27 +177,27 @@
     def _():
         for f in range(4):
             a, b = split_pair(data_ref[:, f].reshape(group * 2 * rows, chunk))
-            high[f], low[f] = a, b
-
-    u, v, h, z = (
-        dot3((inv_ref[0], inv_ref[1]), (high[f], low[f])) for f in range(4)
-    )
+            high[:, f * chunk : (f + 1) * chunk] = a
+            low[:, f * chunk : (f + 1) * chunk] = b
+
+    made = dot3((inv_ref[0], inv_ref[1]), (high[...], low[...]))
+    u, v, h, z = (made[:, f * chunk : (f + 1) * chunk] for f in range(4))
     products = (z * v, z * u, 0.5 * (u * u + v * v), h * u, h * v)
-    for f in range(5):
-        term = dot3((fwd_ref[0], fwd_ref[1]), split_pair(products[f]))
-
-        @pl.when(at == 0)
-        def _():
-            total[f] = term
-
-        @pl.when(at > 0)
-        def _():
-            total[f] = total[f] + term
+    term = dot3((fwd_ref[0], fwd_ref[1]), split_pair(jnp.concatenate(products, axis=1)))
+
+    @pl.when(at == 0)
+    def _():
+        total[...] = term
+
+    @pl.when(at > 0)
+    def _():
+        total[...] = total[...] + term
 
     @pl.when(at == pl.num_programs(0) - 1)
     def _():
         for f in range(5):
-            out_ref[:, f] = total[f].reshape(group, 2, kept, chunk)
+            field = total[:, f * chunk : (f + 1) * chunk]
+            out_ref[:, f] = field.reshape(group, 2, kept, chunk)
 
 
 def middle(data, tables):
@@ -211,18 +217,24 @@
         out_specs=pl.BlockSpec((group, 5, 2, kept, chunk), lambda i: (0, 0, 0, 0, 0)),
         out_shape=jax.ShapeDtypeStruct((group, 5, 2, kept, chunk), jnp.float32),
         scratch_shapes=[
-            pltpu.VMEM((4, group * 2 * rows, chunk), jnp.bfloat16),
-            pltpu.VMEM((4, group * 2 * rows, chunk), jnp.bfloat16),
-            pltpu.VMEM((5, group * 2 * kept, chunk), jnp.float32),
+            pltpu.VMEM((group * 2 * rows, 4 * chunk), jnp.bfloat16),
+            pltpu.VMEM((group * 2 * rows, 4 * chunk), jnp.bfloat16),
+            pltpu.VMEM((group * 2 * kept, 5 * chunk), jnp.float32),
         ],
         compiler_params=pltpu.CompilerParams(vmem_limit_bytes=56 * 1024 * 1024),
+        cost_estimate=pl.CostEstimate(
+            flops=6 * grid_size * chunk * (4 * inv.shape[2] + 5 * fwd.shape[1]),
+            bytes_accessed=4 * (inv.size + fwd.size + 2 * data.size),
+            transcendentals=0,
+        ),
         name="middle",
     )(data, inv, fwd)
 
 
-def forward_kernel(kept_steps, dt, limit, data_ref, state_ref, fac_ref, kx_ref, ky_ref, mat_ref, tw_ref, out_ref):
+def forward_kernel(kept_steps, dt, limit, datas, state_ref, fac_ref, kx_ref, ky_ref, mat_ref, tw_ref, out_ref):
     kx, ky = kx_ref[...], ky_ref[...]
-    group, chunk = data_ref.shape[0], data_ref.shape[4]
+    group, width = datas[0].shape[0], datas[0].shape[4]
+    chunk = width * len(datas)
     rows = ky.shape[0]
     lanes = mat_ref.shape[1] // 2
     factors = (fac_ref[0], fac_ref[1], fac_ref[2])
@@ -244,9 +256,10 @@
         def piece(f, c, k):
             if chunk >= lanes:
                 g, at = divmod(k * lanes, chunk)
-                return data_ref[g, f, c, :, at : at + lanes]
+                o, at = divmod(at, width)
+                return datas[o][g, f, c, :, at : at + lanes]
             per = lanes // chunk
-            return jnp.concatenate([data_ref[k * per + i, f, c] for i in range(per)], axis=1)
+            return jnp.concatenate([datas[0][k * per + i, f, c] for i in range(per)], axis=1)
 
         stacked = jnp.concatenate(
             [
@@ -276,14 +289,18 @@
                 )
             )
         (ar, ai), (br, bi), (kr, ki), (pr, pi), (qr, qi) = modes
-        keep = jnp.where((jnp.abs(kx) <= limit) & (ky <= limit), dt, 0.0)
+        inside = (jnp.abs(kx) <= limit) & (ky <= limit)
+
+        def keep(values):
+            return jnp.where(inside, dt * values, 0.0)
+
         (xr, xi), (yr, yi), (hr, hi) = state
         put(
             apply_parts(
                 (
-                    (xr + keep * (ar + kx * ki), xi + keep * (ai - kx * kr)),
-                    (yr + keep * (ky * ki - br), yi - keep * (bi + ky * kr)),
-                    (hr + keep * (kx * pi + ky * qi), hi - keep * (kx * pr + ky * qr)),
+                    (xr + keep(ar + kx * ki), xi + keep(ai - kx * kr)),
+                    (yr + keep(ky * ki - br), yi - keep(bi + ky * kr)),
+                    (hr + keep(kx * pi + ky * qi), hi - keep(kx * pr + ky * qr)),
                 ),
                 factors,
                 kx,
@@ -292,24 +309,28 @@
         )
 
 
-def forward_x(data, state, tables):
-    group, _, _, kept, chunk = data.shape
+def forward_x(datas, state, tables):
+    group, _, _, kept, width = datas[0].shape
+    count = len(datas)
     _, _, rows, grid_size = state.shape
-    step = 8
-    kept_steps = kept // step
+    step = min(rows, 32)
+    kept_steps = -(-kept // step)
     mat, tw = tables["fwd_x"]
 
     def kernel(*refs):
-        forward_kernel(kept_steps, COURANT / grid_size, float(grid_size // 3), *refs)
+        forward_kernel(kept_steps, COURANT / grid_size, float(grid_size // 3), refs[:count], *refs[count:])
 
     return pl.pallas_call(
         kernel,
         grid=(rows // step,),
         in_specs=[
-            pl.BlockSpec(
-                (group, 5, 2, step, chunk),
-                lambda i: (0, 0, 0, jnp.minimum(i, kept_steps - 1), 0),
-            ),
+            *[
+                pl.BlockSpec(
+                    (group, 5, 2, step, width),
+                    lambda i: (0, 0, 0, jnp.minimum(i, kept_steps - 1), 0),
+                )
+            ]
+            * count,
             pl.BlockSpec((3, 2, step, grid_size), lambda i: (0, 0, i, 0)),
             pl.BlockSpec((3, step, grid_size), lambda i: (0, i, 0)),
             pl.BlockSpec((1, grid_size), lambda i: (0, 0)),
@@ -320,7 +341,7 @@
         out_specs=pl.BlockSpec((3, 2, step, grid_size), lambda i: (0, 0, i, 0)),
         out_shape=jax.ShapeDtypeStruct(state.shape, jnp.float32),
         name="forward_x",
-    )(data, state, tables["factors"], tables["kx"], tables["ky"], mat, tw)
+    )(*datas, state, tables["factors"], tables["kx"], tables["ky"], mat, tw)
 
 
 def scan_kernel(data_ref, fac_ref, kx_ref, ky_ref, out_ref):
@@ -342,7 +363,7 @@
 
 def slab_scan(data, factors, kx, ky):
     slabs, _, _, rows, grid_size = data.shape
-    step = grid_size // 8
+    step = min(grid_size, 128)
     return pl.pallas_call(
         scan_kernel,
         grid=(grid_size // step,),
@@ -390,11 +411,11 @@
 
 
 def fine_step(state, tables):
-    rotated = inverse_x(state, tables)
-    rotated = lax.all_to_all(rotated, GROUP, split_axis=0, concat_axis=0, tiled=True)
-    partial_y = middle(rotated, tables)
-    partial_y = lax.all_to_all(partial_y, GROUP, split_axis=0, concat_axis=0, tiled=True)
-    return forward_x(partial_y, state, tables)
+    def exchange(values):
+        return lax.all_to_all(values, GROUP, split_axis=0, concat_axis=0, tiled=True)
+
+    landed = [exchange(part) for part in inverse_x(state, tables)]
+    return forward_x([exchange(middle(part, tables)) for part in landed], state, tables)
 
 
 def gathered(values, slabs, group, back):
@@ -443,18 +464,30 @@
     current = gathered(jnp.where(own_slab == slabs - 1, init, current), slabs, group, False)
     for _ in range(CF):
         current = fine_step(current, tables)
-    residual = gathered(current, slabs, group, True) - c_state[0]
-
     per = rows // slabs
     start = lax.axis_index(SPACE) * rows + own_slab * per
     ky = (start + jnp.arange(per, dtype=jnp.int32)).astype(jnp.float32)[:, None]
     coarse = prop_factors(float(CF), tables["kx"], ky, grid_size)
-    split = residual.reshape(3, 2, slabs, per, grid_size).transpose(2, 0, 1, 3, 4)
-    split = lax.all_to_all(split, SLAB, split_axis=0, concat_axis=0, tiled=True)
-    split = slab_scan(split, coarse, tables["kx"], ky)
-    split = lax.all_to_all(split, SLAB, split_axis=0, concat_axis=0, tiled=True)
-    moved = split.transpose(1, 2, 0, 3, 4).reshape(residual.shape)
-    return (c_state + moved[None], residual[None])
+    width = grid_size // STREAMS
+    residuals, corrected, held = [], [], None
+    for at in range(STREAMS):
+        lane = slice(at * width, (at + 1) * width)
+        part = current[..., lane]
+        if held is not None:
+            part, held = lax.optimization_barrier((part, held))
+        held = gathered(part, slabs, group, True)
+        residual = held - c_state[0, ..., lane]
+        split = residual.reshape(3, 2, slabs, per, width).transpose(2, 0, 1, 3, 4)
+        split = lax.all_to_all(split, SLAB, split_axis=0, concat_axis=0, tiled=True)
+        split = slab_scan(split, coarse[..., lane], tables["kx"][:, lane], ky)
+        split = lax.all_to_all(split, SLAB, split_axis=0, concat_axis=0, tiled=True)
+        moved = split.transpose(1, 2, 0, 3, 4).reshape(residual.shape)
+        residuals.append(residual)
+        corrected.append(c_state[0, ..., lane] + moved)
+    return (
+        jnp.concatenate(corrected, axis=-1)[None],
+        jnp.concatenate(residuals, axis=-1)[None],
+    )
 
 
 def solution(mesh):

time: 580 us -> 572 us (0.986)
  starting transfers between devices: 63.5 us -> 91.8 us
  blocking collectives: 54 us -> 30.2 us
  waiting for transfers between devices: 260 us -> 245 us
  local copies, waits for them, and re-layouts: 42.7 us -> 56.7 us
  Pallas kernels: 99.7 us -> 85.9 us
    all_to_all x1, blocking collectives: 54 us -> 30.2 us  [exchange(): lax.all_to_all(values, GROUP, split_axis=0, concat_axis=0, tiled=True)]
    all_to_all x2 -> x4, waiting for transfers between devices: 66.9 us -> 50 us  [shards(): split = lax.all_to_all(split, SLAB, split_axis=0, concat_axis=0, tiled=True)]
    all_to_all x3 -> x7, starting transfers between devices: 19.6 us -> 34.4 us  [exchange(): lax.all_to_all(values, GROUP, split_axis=0, concat_axis=0, tiled=True)]
    pallas_call x2, Pallas kernels: 27.1 us -> 15.4 us  [forward_x(): pl.pallas_call(kernel, grid=(rows // step,), in_specs=[*[pl.BlockSpec((gr...]
    all_to_all x3 -> x7, waiting for transfers between devices: 92 us -> 100 us  [exchange(): lax.all_to_all(values, GROUP, split_axis=0, concat_axis=0, tiled=True)]
    ppermute x8 -> x12, starting transfers between devices: 18.4 us -> 26 us  [gathered(): landed.append(lax.ppermute(piece, EVERY, links))]
    slice x0 -> x4, local copies, waits for them, and re-layouts: none -> 6.7 us  [the longest x1 3.33 us: shards(): part = current[..., lane]]
    all_to_all x2 -> x4, starting transfers between devices: 25.5 us -> 31.4 us  [shards(): split = lax.all_to_all(split, SLAB, split_axis=0, concat_axis=0, tiled=True)]
  transfers between devices with their start and end apart: 13 -> 23, of which waited for: 10 -> 17; matrix products, arithmetic and copies ran while one was open for 9% -> 11% of each run, Pallas kernels for 0% -> 10%
where the time goes in v2:
time: 572 us; the launch traced here: 565 us
  waiting for transfers between devices  245 us (43%)
  starting transfers between devices  91.8 us (16%)
  Pallas kernels  85.9 us (15%)
  local copies, waits for them, and re-layouts  56.7 us (10%)
  other arithmetic  53.7 us (9%)
  blocking collectives  30.2 us (5%)
    all_to_all x7, waiting for transfers between devices, exchange(): lax.all_to_all(values, GROUP, split_axis=0, concat_axis=0, tiled=True)  100 us
    ppermute x12, waiting for transfers between devices, gathered(): landed.append(lax.ppermute(piece, EVERY, links))  95 us
    pallas_call x4, Pallas kernels, middle(): pl.pallas_call(middle_kernel, grid=(grid_size // step,), in_specs=[pl.Blo...  50.5 us
    all_to_all x4, waiting for transfers between devices, shards(): split = lax.all_to_all(split, SLAB, split_axis=0, concat_axis=0, tiled=True)  50 us
    all_to_all x7, starting transfers between devices, exchange(): lax.all_to_all(values, GROUP, split_axis=0, concat_axis=0, tiled=True)  34.4 us
    all_to_all x4, starting transfers between devices, shards(): split = lax.all_to_all(split, SLAB, split_axis=0, concat_axis=0, tiled=True)  31.4 us
    all_to_all x1, blocking collectives, exchange(): lax.all_to_all(values, GROUP, split_axis=0, concat_axis=0, tiled=True)  30.2 us
    ppermute x12, starting transfers between devices, gathered(): landed.append(lax.ppermute(piece, EVERY, links))  26 us
  transfers between devices with their start and end apart: 23, of which 17 were waited for; matrix products, arithmetic and copies ran while one was open for 11% of the time, Pallas kernels for 10%

profile of v2, /device:TPU:0, one launch (start us, length us, event | category | flops | bytes accessed | tf_op | source)
XLA Modules:
  0.0 564.8 jit_solution(14883197240649950034)
XLA Ops:
  0.7 4.5 bitcast_select_fusion
  8.3 3.3 constant_dynamic-slice_fusion.3
  12.7 4.1 collective-permute-start
  27.6 33.0 %collective-permute-done = f32[3,2,32,1024]{3,2,1,0:T(8,128)S(1)} collective-permute-done((f32[3,2,32,1024]{3,2,1,0:T(8,128)}, f32[3,2,32,1024]{3,2,1,0:T(8,128)S(1)}, u32[]{:S(2)}, u32[]{:S(2)}) %collective-permute-start) | collective-permute-done | bytes 786464 | tf_op jit(solution)/shard_map/ppermute | solution.py:447
  60.6 21.1 %collective-permute-done.2 = f32[3,2,32,1024]{3,2,1,0:T(8,128)S(1)} collective-permute-done((f32[3,2,32,1024]{3,2,1,0:T(8,128)}, f32[3,2,32,1024]{3,2,1,0:T(8,128)S(1)}, u32[]{:S(2)}, u32[]{:S(2)}) %collective-permute-start.2) | collective-permute-done | bytes 786464 | tf_op jit(solution)/shard_map/ppermute | solution.py:447
  91.5 6.0 %inverse_x.2 = (f32[4,4,2,128,128]{4,3,2,1,0:T(8,128)}, f32[4,4,2,128,128]{4,3,2,1,0:T(8,128)}) custom-call(f32[3,2,128,1024]{3,2,1,0:T(8,128)} %bitcast.82, f32[1,1024]{1,0:T(1,128)} %fusion.41.kx_ref.refs_4_, f32[128,1]{1,0:T(8,128)} %add_convert_fusion.ky_ref.refs_5_, bf16[2,256,256]{2,1,0:T(8,128)(2,1)} %constant.225.mat_ref, ...), custom_call_target="tpu_custom_call" | custom-call | tf_op jit(solution)/shard_map/inverse_x/pallas_call | solution.py:155
  97.5 10.0 %all-to-all-start.2 = ((f32[4,4,2,128,128]{4,3,2,1,0:T(8,128)}), f32[4,4,2,128,128]{4,3,2,1,0:T(8,128)S(1)}, u32[]{:S(2)}, u32[]{:S(2)}) async-start(f32[4,4,2,128,128]{4,3,2,1,0:T(8,128)} %get-tuple-element.9), calls=%async_computation.2 | async-start | bytes 4194304 | tf_op jit(solution)/shard_map/all_to_all | solution.py:415
  107.5 25.7 %all-to-all-done.2.data_ref = f32[4,4,2,128,128]{4,3,2,1,0:T(8,128)S(1)} async-done(((f32[4,4,2,128,128]{4,3,2,1,0:T(8,128)}), f32[4,4,2,128,128]{4,3,2,1,0:T(8,128)S(1)}, u32[]{:S(2)}, u32[]{:S(2)}) %all-to-all-start.2) | async-done | bytes 2097184 | tf_op jit(solution)/shard_map/all_to_all | solution.py:415
  134.6 4.6 all-to-all-start
  139.2 8.3 %cosine_multiply_fusion = (f32[1024,4,1,128]{3,0,2,1:T(8,128)S(1)}, f32[1024,4,1,128]{3,0,2,1:T(8,128)S(1)}) fusion(s32[4,128]{1,0:T(4,128)S(1)} %iota_add_fusion, f32[4,128]{1,0:T(4,128)S(1)} %get-tuple-element.51, f32[4,128]{1,0:T(4,128)S(1)} %get-tuple-element.52), kind=kLoop, calls=%fused_computation.35 | loop fusion | flops 8388608 | bytes 4200448 | tf_op jit(solution)/shard_map/mul | solution.py:399
  147.8 5.5 copy.43
  153.2 6.4 %reshape.744 = f32[1,1024,1024]{2,1,0:T(8,128)} reshape(f32[1024,4,2,128]{3,2,1,0:T(2,128)} %copy.43) | data formatting | bytes 8388608 | tf_op jit(solution)/shard_map/reshape | solution.py:400
  159.6 8.3 %fusion.17 = (f32[4,1,128,1024]{3,2,1,0:T(8,128)S(1)}, f32[4,1,128,1024]{3,2,1,0:T(8,128)S(1)}) fusion(s32[4,128]{1,0:T(4,128)S(1)} %iota_add_fusion), kind=kLoop, calls=%fused_computation.53 | loop fusion | flops 7864320 | bytes 4196352 | tf_op jit(solution)/shard_map/cos | solution.py:394
  175.6 12.9 %middle.5 = f32[4,5,2,88,128]{4,3,2,1,0:T(8,128)} custom-call(f32[4,4,2,128,128]{4,3,2,1,0:T(8,128)} %copy-done.10, bf16[2,1024,1024]{2,1,0:T(8,128)(2,1)} %pad_maximum_fusion.1.inv_ref, bf16[2,704,1024]{2,1,0:T(8,128)(2,1)} %pad_maximum_fusion.4.fwd_ref), custom_call_target="tpu_custom_call" | custom-call | flops 5989466112 | bytes 18350080 | tf_op jit(solution)/shard_map/middle/pallas_call | solution.py:209
  188.5 3.6 all-to-all-start.3
  192.0 12.5 %middle.4 = f32[4,5,2,88,128]{4,3,2,1,0:T(8,128)} custom-call(f32[4,4,2,128,128]{4,3,2,1,0:T(8,128)} %all-to-all-done.data_ref, bf16[2,1024,1024]{2,1,0:T(8,128)(2,1)} %pad_maximum_fusion.1.inv_ref, bf16[2,704,1024]{2,1,0:T(8,128)(2,1)} %pad_maximum_fusion.4.fwd_ref), custom_call_target="tpu_custom_call" | custom-call | flops 5989466112 | bytes 18350080 | tf_op jit(solution)/shard_map/middle/pallas_call | solution.py:209
  204.6 10.0 %all-to-all-done.3.refs_1_ = f32[4,5,2,88,128]{4,3,2,1,0:T(8,128)S(1)} async-done(((f32[4,5,2,88,128]{4,3,2,1,0:T(8,128)}), f32[4,5,2,88,128]{4,3,2,1,0:T(8,128)S(1)}, u32[]{:S(2)}, u32[]{:S(2)}) %all-to-all-start.3) | async-done | bytes 1802272 | tf_op jit(solution)/shard_map/all_to_all | solution.py:415
  214.5 4.5 all-to-all-start.1
  222.6 19.0 %all-to-all-done.1.refs_0_ = f32[4,5,2,88,128]{4,3,2,1,0:T(8,128)} async-done(((f32[4,5,2,88,128]{4,3,2,1,0:T(8,128)}), f32[4,5,2,88,128]{4,3,2,1,0:T(8,128)}, u32[]{:S(2)}, u32[]{:S(2)}) %all-to-all-start.1) | async-done | bytes 1802272 | tf_op jit(solution)/shard_map/all_to_all | solution.py:415
  241.6 7.7 %forward_x.2.state_ref.refs_2_ = f32[3,2,128,1024]{3,2,1,0:T(8,128)} custom-call(f32[4,5,2,88,128]{4,3,2,1,0:T(8,128)} %all-to-all-done.1.refs_0_, f32[4,5,2,88,128]{4,3,2,1,0:T(8,128)} %copy-done.7, f32[3,2,128,1024]{3,2,1,0:T(8,128)} %bitcast.83, f32[3,128,1024]{2,1,0:T(8,128)} %pad_maximum_fusion.5.refs_3_, f32[1,1024]{1,0:T(1,128)} %fusion.41.kx_ref.refs_4_, ...), custom_call_target="tpu_custom_call" | custom-call | tf_op jit(solution)/shard_map/forward_x/pallas_call | solution.py:323
  249.2 6.0 %inverse_x.3 = (f32[4,4,2,128,128]{4,3,2,1,0:T(8,128)}, f32[4,4,2,128,128]{4,3,2,1,0:T(8,128)}) custom-call(f32[3,2,128,1024]{3,2,1,0:T(8,128)} %forward_x.2.state_ref.refs_2_, f32[1,1024]{1,0:T(1,128)} %fusion.41.kx_ref.refs_4_, f32[128,1]{1,0:T(8,128)} %add_convert_fusion.ky_ref.refs_5_, bf16[2,256,256]{2,1,0:T(8,128)(2,1)} %constant.225.mat_ref, ...), custom_call_target="tpu_custom_call" | custom-call | tf_op jit(solution)/shard_map/inverse_x/pallas_call | solution.py:155
  255.2 30.2 %all_to_all.60.data_ref = f32[4,4,2,128,128]{4,3,2,1,0:T(8,128)} all-to-all(f32[4,4,2,128,128]{4,3,2,1,0:T(8,128)} %get-tuple-element.11), channel_id=1, replica_groups=mesh['ta'=4,'core'=2,'zh'=2,'zl'=2] {'core','zl'}, dimensions={0} | all-to-all | bytes 4194304 | tf_op jit(solution)/shard_map/all_to_all | solution.py:415
  285.4 3.8 all-to-all-start.4
  289.2 12.5 %middle.7 = f32[4,5,2,88,128]{4,3,2,1,0:T(8,128)} custom-call(f32[4,4,2,128,128]{4,3,2,1,0:T(8,128)} %all_to_all.60.data_ref, bf16[2,1024,1024]{2,1,0:T(8,128)(2,1)} %pad_maximum_fusion.1.inv_ref, bf16[2,704,1024]{2,1,0:T(8,128)(2,1)} %pad_maximum_fusion.4.fwd_ref), custom_call_target="tpu_custom_call" | custom-call | flops 5989466112 | bytes 18350080 | tf_op jit(solution)/shard_map/middle/pallas_call | solution.py:209
  301.7 13.1 %all-to-all-done.4.data_ref = f32[4,4,2,128,128]{4,3,2,1,0:T(8,128)S(1)} async-done(((f32[4,4,2,128,128]{4,3,2,1,0:T(8,128)}), f32[4,4,2,128,128]{4,3,2,1,0:T(8,128)S(1)}, u32[]{:S(2)}, u32[]{:S(2)}) %all-to-all-start.4) | async-done | bytes 2097184 | tf_op jit(solution)/shard_map/all_to_all | solution.py:415
  316.1 3.6 all-to-all-start.7
  319.7 12.6 %middle.6 = f32[4,5,2,88,128]{4,3,2,1,0:T(8,128)} custom-call(f32[4,4,2,128,128]{4,3,2,1,0:T(8,128)} %copy-done.11, bf16[2,1024,1024]{2,1,0:T(8,128)(2,1)} %pad_maximum_fusion.1.inv_ref, bf16[2,704,1024]{2,1,0:T(8,128)(2,1)} %pad_maximum_fusion.4.fwd_ref), custom_call_target="tpu_custom_call" | custom-call | flops 5989466112 | bytes 18350080 | tf_op jit(solution)/shard_map/middle/pallas_call | solution.py:209
  332.3 9.8 %all-to-all-done.7.refs_1_ = f32[4,5,2,88,128]{4,3,2,1,0:T(8,128)S(1)} async-done(((f32[4,5,2,88,128]{4,3,2,1,0:T(8,128)}), f32[4,5,2,88,128]{4,3,2,1,0:T(8,128)S(1)}, u32[]{:S(2)}, u32[]{:S(2)}) %all-to-all-start.7) | async-done | bytes 1802272 | tf_op jit(solution)/shard_map/all_to_all | solution.py:415
  342.2 4.4 all-to-all-start.5
  346.7 22.5 %all-to-all-done.5.refs_0_ = f32[4,5,2,88,128]{4,3,2,1,0:T(8,128)} async-done(((f32[4,5,2,88,128]{4,3,2,1,0:T(8,128)}), f32[4,5,2,88,128]{4,3,2,1,0:T(8,128)}, u32[]{:S(2)}, u32[]{:S(2)}) %all-to-all-start.5) | async-done | bytes 1802272 | tf_op jit(solution)/shard_map/all_to_all | solution.py:415
  369.1 7.7 %forward_x.3 = f32[3,2,128,1024]{3,2,1,0:T(8,128)} custom-call(f32[4,5,2,88,128]{4,3,2,1,0:T(8,128)} %all-to-all-done.5.refs_0_, f32[4,5,2,88,128]{4,3,2,1,0:T(8,128)} %copy-done.6, f32[3,2,128,1024]{3,2,1,0:T(8,128)} %forward_x.2.state_ref.refs_2_, f32[3,128,1024]{2,1,0:T(8,128)} %pad_maximum_fusion.5.refs_3_, f32[1,1024]{1,0:T(1,128)} %fusion.41.kx_ref.refs_4_, ...), custom_call_target="tpu_custom_call" | custom-call | tf_op jit(solution)/shard_map/forward_x/pallas_call | solution.py:323
  381.2 3.5 collective-permute-start.5
  389.2 5.0 collective-permute-done.5
  394.2 8.4 %collective-permute-done.6 = f32[3,2,32,512]{3,2,1,0:T(8,128)S(1)} collective-permute-done((f32[3,2,32,512]{3,2,1,0:T(8,128)S(1)}, f32[3,2,32,512]{3,2,1,0:T(8,128)S(1)}, u32[]{:S(2)}, u32[]{:S(2)}) %collective-permute-start.6) | collective-permute-done | bytes 393248 | tf_op jit(solution)/shard_map/ppermute | solution.py:447
  402.7 6.1 %collective-permute-done.7 = f32[3,2,32,512]{3,2,1,0:T(8,128)S(1)} collective-permute-done((f32[3,2,32,512]{3,2,1,0:T(8,128)S(1)}, f32[3,2,32,512]{3,2,1,0:T(8,128)S(1)}, u32[]{:S(2)}, u32[]{:S(2)}) %collective-permute-start.7) | collective-permute-done | bytes 393248 | tf_op jit(solution)/shard_map/ppermute | solution.py:447
  419.0 12.4 %all-to-all-start.8 = ((f32[8,3,2,16,512]{4,3,2,1,0:T(8,128)}), f32[8,3,2,16,512]{4,3,2,1,0:T(8,128)}, u32[]{:S(2)}, u32[]{:S(2)}) async-start(f32[8,3,2,16,512]{4,3,2,1,0:T(8,128)} %fusion.16), calls=%async_computation.8 | async-start | bytes 3145728 | tf_op jit(solution)/shard_map/all_to_all | solution.py:481
  433.6 5.8 %collective-permute-start.9 = (f32[3,2,32,512]{3,2,1,0:T(8,128)S(1)}, f32[3,2,32,512]{3,2,1,0:T(8,128)S(1)}, u32[]{:S(2)}, u32[]{:S(2)}) collective-permute-start(f32[3,2,32,512]{3,2,1,0:T(8,128)S(1)} %get-tuple-element.32), channel_id=1, source_target_pairs={{1,0},{4,1},{5,2},{0,3},{3,4},{6,5},{7,6},{2,7},{9,8},{12,9},{13,1... | collective-permute-start | bytes 1179656 | tf_op jit(solution)/shard_map/ppermute | solution.py:447
  441.6 7.2 %collective-permute-done.9 = f32[3,2,32,512]{3,2,1,0:T(8,128)S(1)} collective-permute-done((f32[3,2,32,512]{3,2,1,0:T(8,128)S(1)}, f32[3,2,32,512]{3,2,1,0:T(8,128)S(1)}, u32[]{:S(2)}, u32[]{:S(2)}) %collective-permute-start.9) | collective-permute-done | bytes 393248 | tf_op jit(solution)/shard_map/ppermute | solution.py:447
  448.9 8.4 %collective-permute-done.10 = f32[3,2,32,512]{3,2,1,0:T(8,128)S(1)} collective-permute-done((f32[3,2,32,512]{3,2,1,0:T(8,128)S(1)}, f32[3,2,32,512]{3,2,1,0:T(8,128)S(1)}, u32[]{:S(2)}, u32[]{:S(2)}) %collective-permute-start.10) | collective-permute-done | bytes 393248 | tf_op jit(solution)/shard_map/ppermute | solution.py:447
  457.3 5.8 %collective-permute-done.11 = f32[3,2,32,512]{3,2,1,0:T(8,128)S(1)} collective-permute-done((f32[3,2,32,512]{3,2,1,0:T(8,128)S(1)}, f32[3,2,32,512]{3,2,1,0:T(8,128)S(1)}, u32[]{:S(2)}, u32[]{:S(2)}) %collective-permute-start.11) | collective-permute-done | bytes 393248 | tf_op jit(solution)/shard_map/ppermute | solution.py:447
  473.3 10.5 %all-to-all-start.10 = ((f32[8,3,2,16,512]{4,3,2,1,0:T(8,128)}), f32[8,3,2,16,512]{4,3,2,1,0:T(8,128)}, u32[]{:S(2)}, u32[]{:S(2)}) async-start(f32[8,3,2,16,512]{4,3,2,1,0:T(8,128)} %fusion.15), calls=%async_computation.10 | async-start | bytes 3145728 | tf_op jit(solution)/shard_map/all_to_all | solution.py:481
  486.1 3.9 slab_scan.2
  490.0 14.9 %all-to-all-done.10.data_ref = f32[8,3,2,16,512]{4,3,2,1,0:T(8,128)} async-done(((f32[8,3,2,16,512]{4,3,2,1,0:T(8,128)}), f32[8,3,2,16,512]{4,3,2,1,0:T(8,128)}, u32[]{:S(2)}, u32[]{:S(2)}) %all-to-all-start.10) | async-done | bytes 1572896 | tf_op jit(solution)/shard_map/all_to_all | solution.py:481
  504.9 4.3 all-to-all-start.9
  509.2 4.1 slab_scan.3
  513.3 16.9 %all-to-all-done.9 = f32[8,3,2,16,512]{4,3,2,1,0:T(8,128)} async-done(((f32[8,3,2,16,512]{4,3,2,1,0:T(8,128)}), f32[8,3,2,16,512]{4,3,2,1,0:T(8,128)}, u32[]{:S(2)}, u32[]{:S(2)}) %all-to-all-start.9) | async-done | bytes 1572896 | tf_op jit(solution)/shard_map/all_to_all | solution.py:483
  530.2 4.3 all-to-all-start.11
  537.3 18.2 %all-to-all-done.11 = f32[8,3,2,16,512]{4,3,2,1,0:T(8,128)} async-done(((f32[8,3,2,16,512]{4,3,2,1,0:T(8,128)}), f32[8,3,2,16,512]{4,3,2,1,0:T(8,128)}, u32[]{:S(2)}, u32[]{:S(2)}) %all-to-all-start.11) | async-done | bytes 1572896 | tf_op jit(solution)/shard_map/all_to_all | solution.py:483
  (103 shorter events, 86.6 us)
Async XLA Ops:
  12.7 47.9 %collective-permute-start = (f32[3,2,32,1024]{3,2,1,0:T(8,128)}, f32[3,2,32,1024]{3,2,1,0:T(8,128)S(1)}, u32[]{:S(2)}, u32[]{:S(2)}) collective-permute-start(f32[3,2,32,1024]{3,2,1,0:T(8,128)} %bitcast.81), channel_id=1, source_target_pairs={{0,2},{1,3},{2,6},{3,7},{4,8},{5,9},{6,12},{7,13},{8,10},{9,11},{1... | collective-permute-start | bytes 2359304 | tf_op jit(solution)/shard_map/ppermute | solution.py:447
  17.8 42.8 %collective-permute-start.1 = (f32[3,2,32,1024]{3,2,1,0:T(8,128)}, f32[3,2,32,1024]{3,2,1,0:T(8,128)S(1)}, u32[]{:S(2)}, u32[]{:S(2)}) collective-permute-start(f32[3,2,32,1024]{3,2,1,0:T(8,128)} %bitcast.80), channel_id=1, source_target_pairs={{0,3},{1,6},{2,7},{3,2},{4,9},{5,12},{6,13},{7,8},{8,11},{9,14},{1... | collective-permute-start | bytes 2359304 | tf_op jit(solution)/shard_map/ppermute | solution.py:447
  19.9 61.8 %collective-permute-start.2 = (f32[3,2,32,1024]{3,2,1,0:T(8,128)}, f32[3,2,32,1024]{3,2,1,0:T(8,128)S(1)}, u32[]{:S(2)}, u32[]{:S(2)}) collective-permute-start(f32[3,2,32,1024]{3,2,1,0:T(8,128)} %bitcast.79), channel_id=1, source_target_pairs={{0,6},{1,7},{2,2},{3,3},{4,12},{5,13},{6,8},{7,9},{8,14},{9,15},{1... | collective-permute-start | bytes 2359304 | tf_op jit(solution)/shard_map/ppermute | solution.py:447
  24.1 57.6 %collective-permute-start.3 = (f32[3,2,32,1024]{3,2,1,0:T(8,128)}, f32[3,2,32,1024]{3,2,1,0:T(8,128)S(1)}, u32[]{:S(2)}, u32[]{:S(2)}) collective-permute-start(f32[3,2,32,1024]{3,2,1,0:T(8,128)} %bitcast.78), channel_id=1, source_target_pairs={{0,7},{1,2},{2,3},{3,6},{4,13},{5,8},{6,9},{7,12},{8,15},{9,10},{1... | collective-permute-start | bytes 2359304 | tf_op jit(solution)/shard_map/ppermute | solution.py:447
  60.6 21.1 %copy-start.12 = (f32[3,2,32,1024]{3,2,1,0:T(8,128)}, f32[3,2,32,1024]{3,2,1,0:T(8,128)S(1)}, u32[]{:S(2)}) copy-start(f32[3,2,32,1024]{3,2,1,0:T(8,128)S(1)} %collective-permute-done) | copy-start | bytes 2359300
  60.6 21.1 %copy-start.13 = (f32[3,2,32,1024]{3,2,1,0:T(8,128)}, f32[3,2,32,1024]{3,2,1,0:T(8,128)S(1)}, u32[]{:S(2)}) copy-start(f32[3,2,32,1024]{3,2,1,0:T(8,128)S(1)} %collective-permute-done.1) | copy-start | bytes 2359300
  81.7 0.9 copy-start.14
  81.7 1.1 copy-start.15
  97.5 35.7 %all-to-all-start.2 = ((f32[4,4,2,128,128]{4,3,2,1,0:T(8,128)}), f32[4,4,2,128,128]{4,3,2,1,0:T(8,128)S(1)}, u32[]{:S(2)}, u32[]{:S(2)}) async-start(f32[4,4,2,128,128]{4,3,2,1,0:T(8,128)} %get-tuple-element.9), calls=%async_computation.2 | async-start | bytes 4194304 | tf_op jit(solution)/shard_map/all_to_all | solution.py:415
  133.2 1.4 copy-start.10
  134.6 53.9 %all-to-all-start = ((f32[4,4,2,128,128]{4,3,2,1,0:T(8,128)}), f32[4,4,2,128,128]{4,3,2,1,0:T(8,128)}, u32[]{:S(2)}, u32[]{:S(2)}) async-start(f32[4,4,2,128,128]{4,3,2,1,0:T(8,128)} %get-tuple-element.8), calls=%async_computation | async-start | bytes 4194304 | tf_op jit(solution)/shard_map/all_to_all | solution.py:415
  169.0 3.2 copy-start.1
  188.5 26.1 %all-to-all-start.3 = ((f32[4,5,2,88,128]{4,3,2,1,0:T(8,128)}), f32[4,5,2,88,128]{4,3,2,1,0:T(8,128)S(1)}, u32[]{:S(2)}, u32[]{:S(2)}) async-start(f32[4,5,2,88,128]{4,3,2,1,0:T(8,128)} %middle.5), calls=%async_computation.3 | async-start | bytes 3604480 | tf_op jit(solution)/shard_map/all_to_all | solution.py:415
  214.5 6.7 %copy-start.7 = (f32[4,5,2,88,128]{4,3,2,1,0:T(8,128)}, f32[4,5,2,88,128]{4,3,2,1,0:T(8,128)S(1)}, u32[]{:S(2)}) copy-start(f32[4,5,2,88,128]{4,3,2,1,0:T(8,128)S(1)} %all-to-all-done.3.refs_1_) | copy-start | bytes 5406724
  214.5 27.0 %all-to-all-start.1 = ((f32[4,5,2,88,128]{4,3,2,1,0:T(8,128)}), f32[4,5,2,88,128]{4,3,2,1,0:T(8,128)}, u32[]{:S(2)}, u32[]{:S(2)}) async-start(f32[4,5,2,88,128]{4,3,2,1,0:T(8,128)} %middle.4), calls=%async_computation.1 | async-start | bytes 3604480 | tf_op jit(solution)/shard_map/all_to_all | solution.py:415
  285.4 29.4 %all-to-all-start.4 = ((f32[4,4,2,128,128]{4,3,2,1,0:T(8,128)}), f32[4,4,2,128,128]{4,3,2,1,0:T(8,128)S(1)}, u32[]{:S(2)}, u32[]{:S(2)}) async-start(f32[4,4,2,128,128]{4,3,2,1,0:T(8,128)} %get-tuple-element.10), calls=%async_computation.4 | async-start | bytes 4194304 | tf_op jit(solution)/shard_map/all_to_all | solution.py:415
  314.8 1.3 copy-start.11
  316.1 26.1 %all-to-all-start.7 = ((f32[4,5,2,88,128]{4,3,2,1,0:T(8,128)}), f32[4,5,2,88,128]{4,3,2,1,0:T(8,128)S(1)}, u32[]{:S(2)}, u32[]{:S(2)}) async-start(f32[4,5,2,88,128]{4,3,2,1,0:T(8,128)} %middle.7), calls=%async_computation.7 | async-start | bytes 3604480 | tf_op jit(solution)/shard_map/all_to_all | solution.py:415
  342.2 27.0 %copy-start.6 = (f32[4,5,2,88,128]{4,3,2,1,0:T(8,128)}, f32[4,5,2,88,128]{4,3,2,1,0:T(8,128)S(1)}, u32[]{:S(2)}) copy-start(f32[4,5,2,88,128]{4,3,2,1,0:T(8,128)S(1)} %all-to-all-done.7.refs_1_) | copy-start | bytes 5406724
  342.2 27.0 %all-to-all-start.5 = ((f32[4,5,2,88,128]{4,3,2,1,0:T(8,128)}), f32[4,5,2,88,128]{4,3,2,1,0:T(8,128)}, u32[]{:S(2)}, u32[]{:S(2)}) async-start(f32[4,5,2,88,128]{4,3,2,1,0:T(8,128)} %middle.6), calls=%async_computation.5 | async-start | bytes 3604480 | tf_op jit(solution)/shard_map/all_to_all | solution.py:415
  380.2 6.9 %copy-start = (f32[1,3,2,128,1024]{4,3,2,1,0:T(8,128)S(1)}, f32[1,3,2,128,1024]{4,3,2,1,0:T(8,128)}, u32[]{:S(2)}) copy-start(f32[1,3,2,128,1024]{4,3,2,1,0:T(8,128)} %param.8) | copy-start | bytes 9437188
  380.4 8.8 %collective-permute-start.4 = (f32[3,2,32,512]{3,2,1,0:T(8,128)S(1)}, f32[3,2,32,512]{3,2,1,0:T(8,128)S(1)}, u32[]{:S(2)}, u32[]{:S(2)}) collective-permute-start(f32[3,2,32,512]{3,2,1,0:T(8,128)S(1)} %get-tuple-element.33), channel_id=1, source_target_pairs={{0,0},{1,1},{4,2},{5,3},{2,4},{3,5},{6,6},{7,7},{8,8},{9,9},{12,10... | collective-permute-start | bytes 1179656 | tf_op jit(solution)/shard_map/ppermute | solution.py:447
  381.2 13.0 %collective-permute-start.5 = (f32[3,2,32,512]{3,2,1,0:T(8,128)S(1)}, f32[3,2,32,512]{3,2,1,0:T(8,128)S(1)}, u32[]{:S(2)}, u32[]{:S(2)}) collective-permute-start(f32[3,2,32,512]{3,2,1,0:T(8,128)S(1)} %get-tuple-element.36), channel_id=1, source_target_pairs={{1,0},{4,1},{5,2},{0,3},{3,4},{6,5},{7,6},{2,7},{9,8},{12,9},{13,1... | collective-permute-start | bytes 1179656 | tf_op jit(solution)/shard_map/ppermute | solution.py:447
  384.7 17.9 %collective-permute-start.6 = (f32[3,2,32,512]{3,2,1,0:T(8,128)S(1)}, f32[3,2,32,512]{3,2,1,0:T(8,128)S(1)}, u32[]{:S(2)}, u32[]{:S(2)}) collective-permute-start(f32[3,2,32,512]{3,2,1,0:T(8,128)S(1)} %get-tuple-element.35), channel_id=1, source_target_pairs={{4,0},{5,1},{0,2},{1,3},{6,4},{7,5},{2,6},{3,7},{12,8},{13,9},{8,1... | collective-permute-start | bytes 1179656 | tf_op jit(solution)/shard_map/ppermute | solution.py:447
  384.7 24.0 %collective-permute-start.7 = (f32[3,2,32,512]{3,2,1,0:T(8,128)S(1)}, f32[3,2,32,512]{3,2,1,0:T(8,128)S(1)}, u32[]{:S(2)}, u32[]{:S(2)}) collective-permute-start(f32[3,2,32,512]{3,2,1,0:T(8,128)S(1)} %get-tuple-element.34), channel_id=1, source_target_pairs={{5,0},{0,1},{1,2},{4,3},{7,4},{2,5},{3,6},{6,7},{13,8},{8,9},{9,10... | collective-permute-start | bytes 1179656 | tf_op jit(solution)/shard_map/ppermute | solution.py:447
  414.9 2.4 copy-start.9
  416.1 1.1 copy-start.2
  419.0 54.4 %all-to-all-start.8 = ((f32[8,3,2,16,512]{4,3,2,1,0:T(8,128)}), f32[8,3,2,16,512]{4,3,2,1,0:T(8,128)}, u32[]{:S(2)}, u32[]{:S(2)}) async-start(f32[8,3,2,16,512]{4,3,2,1,0:T(8,128)} %fusion.16), calls=%async_computation.8 | async-start | bytes 3145728 | tf_op jit(solution)/shard_map/all_to_all | solution.py:481
  432.9 8.8 %collective-permute-start.8 = (f32[3,2,32,512]{3,2,1,0:T(8,128)S(1)}, f32[3,2,32,512]{3,2,1,0:T(8,128)S(1)}, u32[]{:S(2)}, u32[]{:S(2)}) collective-permute-start(f32[3,2,32,512]{3,2,1,0:T(8,128)S(1)} %get-tuple-element.29), channel_id=1, source_target_pairs={{0,0},{1,1},{4,2},{5,3},{2,4},{3,5},{6,6},{7,7},{8,8},{9,9},{12,10... | collective-permute-start | bytes 1179656 | tf_op jit(solution)/shard_map/ppermute | solution.py:447
  433.6 15.3 %collective-permute-start.9 = (f32[3,2,32,512]{3,2,1,0:T(8,128)S(1)}, f32[3,2,32,512]{3,2,1,0:T(8,128)S(1)}, u32[]{:S(2)}, u32[]{:S(2)}) collective-permute-start(f32[3,2,32,512]{3,2,1,0:T(8,128)S(1)} %get-tuple-element.32), channel_id=1, source_target_pairs={{1,0},{4,1},{5,2},{0,3},{3,4},{6,5},{7,6},{2,7},{9,8},{12,9},{13,1... | collective-permute-start | bytes 1179656 | tf_op jit(solution)/shard_map/ppermute | solution.py:447
  439.3 17.9 %collective-permute-start.10 = (f32[3,2,32,512]{3,2,1,0:T(8,128)S(1)}, f32[3,2,32,512]{3,2,1,0:T(8,128)S(1)}, u32[]{:S(2)}, u32[]{:S(2)}) collective-permute-start(f32[3,2,32,512]{3,2,1,0:T(8,128)S(1)} %get-tuple-element.31), channel_id=1, source_target_pairs={{4,0},{5,1},{0,2},{1,3},{6,4},{7,5},{2,6},{3,7},{12,8},{13,9},{8,1... | collective-permute-start | bytes 1179656 | tf_op jit(solution)/shard_map/ppermute | solution.py:447
  439.4 23.7 %collective-permute-start.11 = (f32[3,2,32,512]{3,2,1,0:T(8,128)S(1)}, f32[3,2,32,512]{3,2,1,0:T(8,128)S(1)}, u32[]{:S(2)}, u32[]{:S(2)}) collective-permute-start(f32[3,2,32,512]{3,2,1,0:T(8,128)S(1)} %get-tuple-element.30), channel_id=1, source_target_pairs={{5,0},{0,1},{1,2},{4,3},{7,4},{2,5},{3,6},{6,7},{13,8},{8,9},{9,10... | collective-permute-start | bytes 1179656 | tf_op jit(solution)/shard_map/ppermute | solution.py:447
  469.3 2.4 copy-start.8
  470.5 1.2 copy-start.4
  473.3 11.4 %copy-start.16 = (f32[1,1024]{1,0:T(1,128)S(1)}, f32[1,1024]{1,0:T(1,128)}, u32[]{:S(2)}) copy-start(f32[1,1024]{1,0:T(1,128)} %fusion.41.kx_ref.refs_4_) | copy-start | bytes 12292
  473.3 31.6 %all-to-all-start.10 = ((f32[8,3,2,16,512]{4,3,2,1,0:T(8,128)}), f32[8,3,2,16,512]{4,3,2,1,0:T(8,128)}, u32[]{:S(2)}, u32[]{:S(2)}) async-start(f32[8,3,2,16,512]{4,3,2,1,0:T(8,128)} %fusion.15), calls=%async_computation.10 | async-start | bytes 3145728 | tf_op jit(solution)/shard_map/all_to_all | solution.py:481
  504.9 25.3 %all-to-all-start.9 = ((f32[8,3,2,16,512]{4,3,2,1,0:T(8,128)}), f32[8,3,2,16,512]{4,3,2,1,0:T(8,128)}, u32[]{:S(2)}, u32[]{:S(2)}) async-start(f32[8,3,2,16,512]{4,3,2,1,0:T(8,128)} %slab_scan.2), calls=%async_computation.9 | async-start | bytes 3145728 | tf_op jit(solution)/shard_map/all_to_all | solution.py:483
  530.2 25.3 %all-to-all-start.11 = ((f32[8,3,2,16,512]{4,3,2,1,0:T(8,128)}), f32[8,3,2,16,512]{4,3,2,1,0:T(8,128)}, u32[]{:S(2)}, u32[]{:S(2)}) async-start(f32[8,3,2,16,512]{4,3,2,1,0:T(8,128)} %slab_scan.3), calls=%async_computation.11 | async-start | bytes 3145728 | tf_op jit(solution)/shard_map/all_to_all | solution.py:483
  555.5 1.9 copy-start.3
  555.5 2.4 copy-start.5
